TPU v7x, 512 devices: a whole 4x8x8 slice. The times are simulated.
512 devices in a mesh: samp: 32 (over x, z), blk: 16 (over y, core).
Axes of the slice: x: 4, y: 8, z: 8, core: 2. Of those that a mesh axis runs over, the one named last changes fastest.
Arguments:
- dosages: int32 [49152, 8192], P('samp', 'blk'), may hold values from 0 to 2, as said below
- new_dosages: int32 [49152, 2048], P('samp', 'blk'), may hold values from 0 to 2, as said below
- traits: float32 [64, 49152], P(None, 'samp'), may hold values from -40 to 40
- shrink: float32 [5], replicated, may hold values from 0.5 to 5
Outputs:
- residual: float32 [5, 64, 49152], P(None, 'blk', 'samp')
- scores: float32 [5, 64, 2048], P(None, None, 'blk')
Inputs may be any that keep to these rules, and one draw needn't show every extreme that they name: `dosages`: codes of haplotype pairs, with linkage along neighbouring variants. `new_dosages`: codes of haplotype pairs, with linkage along neighbouring variants.
All inputs are finite; a program needn't handle non-finite values.
Results may differ from a plain program's by a relative error of at most 0.0053.
Values may be sent and summed in bfloat16 or wider, within the bound.
No kernel may reach another device: no remote copies, remote signals or barrier semaphores. Data moves between devices by JAX's collectives and lax.ppermute only.
A program may use at most 64 MiB of HBM per device.

v0:
```python
import jax
import jax.numpy as jnp
from jax import lax
from jax.sharding import PartitionSpec as P

RIDGE = 5
CHEB = 3


def chebyshev(rhs_cols, apply_fn, centre, half_width, sweeps):
    sig_ratio = centre / half_width
    factor = 1.0 / sig_ratio
    direction = rhs_cols / centre
    iterate = jnp.zeros_like(rhs_cols)
    remain = rhs_cols
    for sweep_index in range(sweeps):
        iterate = iterate + direction
        if sweep_index + 1 < sweeps:
            remain = remain - apply_fn(direction)
            factor_next = 1.0 / (2.0 * sig_ratio - factor)
            direction = factor_next * factor * direction + 2.0 * factor_next / half_width * remain
            factor = factor_next
    return iterate


def scaled(values, column_sum, column_sq, count):
    column_mean = column_sum / count
    column_var = column_sq / count - column_mean * column_mean
    inverse = 1.0 / jnp.sqrt(column_var + 1e-05)
    return ((values - column_mean) * inverse).astype(jnp.bfloat16)


def shards(dosages, new_dosages, traits, shrink):
    local_rows = dosages.shape[0]
    trait_count = traits.shape[0]
    count = float(local_rows * lax.axis_size("samp"))
    block_codes = dosages.astype(jnp.float32)
    new_codes = new_dosages.astype(jnp.float32)
    block_sum, block_sq, new_sum, new_sq = lax.psum(
        (
            jnp.sum(block_codes, axis=0),
            jnp.sum(block_codes * block_codes, axis=0),
            jnp.sum(new_codes, axis=0),
            jnp.sum(new_codes * new_codes, axis=0),
        ),
        "samp",
    )
    standard = scaled(block_codes, block_sum, block_sq, count)
    fresh = scaled(new_codes, new_sum, new_sq, count)
    trait_bf = traits.astype(jnp.bfloat16)
    gram = lax.dot_general(
        standard, standard, (((0,), (0,)), ((), ())), preferred_element_type=jnp.float32
    )
    cross = lax.dot_general(
        standard, trait_bf, (((0,), (1,)), ((), ())), preferred_element_type=jnp.float32
    )
    lam_cols = jnp.repeat(shrink, trait_count)
    gram_full, cross_full = lax.psum((gram, cross), "samp")
    bound = jnp.max(jnp.sum(jnp.abs(gram_full), axis=0)) / count

    def apply_full(direction):
        return (
            jnp.dot(gram_full, direction, precision=lax.Precision.HIGHEST) / count
            + lam_cols * direction
        )

    rhs_cols = jnp.tile(cross_full / count, (1, RIDGE))
    weights = chebyshev(
        rhs_cols, apply_full, lam_cols + bound / 2.0, bound / 2.0 + jnp.zeros_like(lam_cols), CHEB
    )
    weight_bf = weights.astype(jnp.bfloat16)
    pred = lax.dot_general(
        weight_bf, standard, (((0,), (1,)), ((), ())), preferred_element_type=jnp.float32
    )
    pred = pred.reshape(RIDGE, trait_count, local_rows)
    share = trait_count // lax.axis_size("blk")
    pred_part = lax.psum_scatter(pred, "blk", scatter_dimension=1, tiled=True)
    own_traits = lax.dynamic_slice_in_dim(traits, lax.axis_index("blk") * share, share, 0)
    residual = own_traits[None, :, :] - pred_part
    res_bf = lax.all_gather(residual.astype(jnp.bfloat16), "blk", axis=1, tiled=True)
    res_flat = res_bf.reshape(RIDGE * trait_count, local_rows)
    raw_part = jnp.dot(res_flat, fresh, preferred_element_type=jnp.float32)
    res_float = res_flat.astype(jnp.float32)
    raw, sum_sq = lax.psum((raw_part, jnp.sum(res_float * res_float, axis=1)), "samp")
    scores = raw / jnp.sqrt(count * (sum_sq / count + 1e-05))[:, None]
    return (residual, scores.reshape(RIDGE, trait_count, fresh.shape[1]))


def solution(mesh):
    placed = (P("samp", "blk"), P("samp", "blk"), P(None, "samp"), P())
    return jax.shard_map(
        shards,
        mesh=mesh,
        in_specs=placed,
        out_specs=(P(None, "blk", "samp"), P(None, None, "blk")),
        check_vma=False,
    )
```

profile of v0, /device:TPU:40, one launch (start us, length us, event | category | flops | bytes accessed | tf_op | source)
XLA Modules:
  0.0 635.2 jit_solution(12466145692508958539)
XLA Ops:
  7.2 0.0 all-reduce.12.cloned.1.call-start
  7.2 2.4 convert_reduce_fusion
  9.6 80.8 %all-reduce.2 = (f32[512]{0:T(512)S(1)}, f32[512]{0:T(512)S(1)}) all-reduce(f32[512]{0:T(512)S(1)} %get-tuple-element.3, f32[512]{0:T(512)S(1)} %get-tuple-element.2), channel_id=1, replica_groups=mesh['samp'=32,'blk'=16] {'samp'}, use_global_device_ids=true, to_apply=%region_3.0 | all-reduce | flops 1024 | bytes 8192 | tf_op jit(solution)/shard_map/psum | solution.py:39
  90.4 2.3 multiply_convert_fusion
  92.8 0.0 copy-start.2
  92.8 2.0 fusion.21
  94.8 0.0 copy-done.2
  94.8 0.0 copy-start.3
  94.8 1.0 fusion.16
  95.9 0.0 all-reduce.12.cloned.1.call-update
  95.9 0.0 all-reduce.10.cloned.1.call-start
  95.9 0.0 copy-done.3
  96.0 0.1 broadcast_in_dim.2
  96.0 0.1 reshape.58
  96.1 155.7 %all-reduce.12.cloned.1.call-done = (f32[512,64]{0,1:T(8,128)}, f32[512,512]{1,0:T(8,128)}) async-done(((f32[512,64]{0,1:T(8,128)}, f32[512,512]{1,0:T(8,128)}), (f32[512,64]{0,1:T(8,128)}, f32[512,512]{1,0:T(8,128)})) %all-reduce.12.cloned.1.call-update) | async-done | bytes 1179664 | tf_op jit(solution)/shard_map/psum | solution.py:58
  251.8 0.0 copy-start
  251.8 1.5 abs_reduce_fusion
  253.3 0.6 reduce_max.9
  254.6 0.9 broadcast_multiply_fusion
  255.5 0.1 bitcast_divide_fusion
  255.6 0.1 tile.4
  255.7 0.0 copy-done
  255.7 1.3 fusion.6
  257.1 1.6 fusion.7
  258.7 2.0 fusion.22
  260.7 0.0 copy-start.1
  260.7 0.0 all-reduce.10.cloned.1.call-update
  260.7 0.0 all-reduce.8.cloned.1.call-start
  260.8 1.3 dynamic-slice
  262.8 0.0 copy-done.1
  262.8 0.2 convert_reduce_fusion.1
  263.0 113.0 %all-reduce.10.cloned.1.call-done = f32[5,64,1536]{2,1,0:T(8,128)} async-done(((f32[5,64,1536]{2,1,0:T(8,128)}), f32[5,64,1536]{2,1,0:T(8,128)}) %all-reduce.10.cloned.1.call-update) | async-done | bytes 1966096
  376.0 1.6 fusion.20
  377.7 21.2 %all_gather.3 = bf16[5,64,1536]{2,0,1:T(8,128)(2,1)S(1)} all-gather(bf16[5,4,1536]{2,0,1:T(8,128)(2,1)S(1)} %copy.11), channel_id=1, replica_groups=mesh['samp'=32,'blk'=16] {'blk'}, dimensions={1}, use_global_device_ids=true | all-gather | bytes 1044480 | tf_op jit(solution)/shard_map/all_gather | solution.py:80
  398.9 0.5 multiply_reduce_fusion
  399.4 0.3 copy.12
  399.7 0.1 copy.13
  399.8 0.1 reduce_sum.62
  399.9 75.7 %all-reduce.1 = (f32[128]{0:T(128)S(1)}, f32[128]{0:T(128)S(1)}, f32[320]{0:T(512)S(1)}) all-reduce(f32[128]{0:T(128)S(1)} %get-tuple-element.5, f32[128]{0:T(128)S(1)} %get-tuple-element.4, f32[320]{0:T(512)S(1)} %reduce_sum.62), channel_id=1, replica_groups=mesh['samp'=32,'blk'=16] {'samp'}, use_global_device_ids=true, to_apply=%region_12.0 | all-reduce | flops 576 | bytes 4608 | tf_op jit(solution)/shard_map/psum | solution.py:39
  475.6 1.1 fusion.11
  476.7 0.0 all-reduce.8.cloned.1.call-update
  476.7 150.3 %all-reduce.8.cloned.1.call-done = f32[320,128]{1,0:T(8,128)} async-done(((f32[320,128]{1,0:T(8,128)}), f32[320,128]{1,0:T(8,128)}) %all-reduce.8.cloned.1.call-update) | async-done | bytes 163856 | tf_op jit(solution)/shard_map/psum | solution.py:84
  627.0 1.7 broadcast_divide_fusion
  (7 shorter events, 0.1 us)
Async XLA Ops:
  7.2 244.7 %all-reduce.12.cloned.1.call-start = ((), (), s32[]{:S(2)}) async-start(), calls=%async_computation.2 | async-start | bytes 2359296 | tf_op jit(solution)/shard_map/psum | solution.py:58
  92.8 2.1 copy-start.2
  94.8 1.1 copy-start.3
  95.9 280.1 %all-reduce.10.cloned.1.call-start = ((), (), s32[]{:S(2)}) async-start(), calls=%async_computation.1 | async-start | bytes 3932160
  251.8 3.9 copy-start
  260.7 2.1 copy-start.1
  260.7 366.3 %all-reduce.8.cloned.1.call-start = ((), (), s32[]{:S(2)}) async-start(), calls=%async_computation | async-start | bytes 327680 | tf_op jit(solution)/shard_map/psum | solution.py:84
Sparse Core Ops, SparseCore 0:
  96.0 155.7 all-reduce.11
  260.9 115.1 all-reduce.9
  476.8 150.1 all-reduce.7
where the time goes:
time: 636 us; the launch traced here: 635 us
  waiting for transfers between devices  419 us (66%)
  blocking collectives  178 us (28%)
  between operations  15.2 us (2%)
  other arithmetic  11.9 us (2%)
  matrix products  9.16 us (1%)
    psum x2, blocking collectives, shards(): lax.psum((jnp.sum(block_codes, axis=0), jnp.sum(block_codes * block_codes...  157 us
    psum x1, waiting for transfers between devices, shards(): gram_full, cross_full = lax.psum((gram, cross), 'samp')  156 us
    psum x1, waiting for transfers between devices, shards(): lax.psum((raw_part, jnp.sum(res_float * res_float, axis=1)), 'samp')  150 us
    unnamed x4, waiting for transfers between devices  113 us
    all_gather x1, blocking collectives, shards(): lax.all_gather(residual.astype(jnp.bfloat16), 'blk', axis=1, tiled=True)  21.2 us
  transfers between devices with their start and end apart: 3, of which 3 were waited for; matrix products, arithmetic and copies ran while one was open for 0% of the time, Pallas kernels for 0%

commit v1 on v0

v1 whole, which is shorter than its diff:
```python
import jax
import jax.numpy as jnp
from jax import lax
from jax.sharding import Mesh, PartitionSpec as P

RIDGE = 5
SAMP = ("x", "z")
BLK = ("y", "core")
FACTORS = {32: (4, 8), 16: (8, 2), 4: (2, 2)}
EPS = 1e-05
F32 = jnp.float32
BF16 = jnp.bfloat16


def dot(a, b, contract, precision=None):
    return lax.dot_general(
        a, b, (contract, ((), ())), precision=precision, preferred_element_type=F32
    )


def rounded(values):
    return lax.reduce_precision(values, 8, 7)


def column_stats(shifted_sum, shifted_sq, count):
    mean = (shifted_sum + count) / count
    var = (shifted_sq + 2.0 * shifted_sum + count) / count - mean * mean
    return mean, 1.0 / jnp.sqrt(var + EPS)


def scaled(codes, mean, inv):
    return ((codes.astype(F32) - mean) * inv).astype(BF16)


def affine(shifted_sum, shifted_sq, mean, inv, count):
    low, mid, high = (rounded((code - mean) * inv) for code in (0.0, 1.0, 2.0))
    n_low = (shifted_sq - shifted_sum) * 0.5
    n_high = (shifted_sq + shifted_sum) * 0.5
    n_mid = count - shifted_sq
    value_mean = (n_low * low + n_mid * mid + n_high * high) / count
    pairs = n_low * n_mid + n_mid * n_high + 4.0 * n_low * n_high
    slopes = (
        n_low * n_mid * (mid - low)
        + n_mid * n_high * (high - mid)
        + 2.0 * n_low * n_high * (high - low)
    )
    slope = jnp.where(pairs > 0.0, slopes / jnp.maximum(pairs, 1.0), inv)
    square = (n_low * low * low + n_mid * mid * mid + n_high * high * high) / count
    return value_mean, slope, square


def chebyshev_coefficients(lam, bound):
    centre = lam + bound / 2.0
    half = bound / 2.0
    sig = centre / half
    q0 = 1.0 / sig
    d0 = 1.0 / centre
    r1a, r1b = 1.0 - lam * d0, -d0
    q1 = 1.0 / (2.0 * sig - q0)
    step = 2.0 * q1 / half
    d1a, d1b = q1 * q0 * d0 + step * r1a, step * r1b
    r2a = r1a - lam * d1a
    r2b = r1b - d1a - lam * d1b
    r2c = -d1b
    q2 = 1.0 / (2.0 * sig - q1)
    step = 2.0 * q2 / half
    d2a, d2b, d2c = q2 * q1 * d1a + step * r2a, q2 * q1 * d1b + step * r2b, step * r2c
    return d0 + d1a + d2a, d1b + d2b, d2c


def shards(dosages, new_dosages, traits, shrink):
    rows, width = dosages.shape
    fresh_width = new_dosages.shape[1]
    trait_count = traits.shape[0]
    samp, blk = lax.axis_size(SAMP), lax.axis_size(BLK)
    depth, cores, zs = lax.axis_size("y"), lax.axis_size("core"), lax.axis_size("z")
    count = float(rows * samp)
    half_width = width // 2
    share_rows = half_width // samp
    share = trait_count // blk
    columns = RIDGE * trait_count

    codes = (dosages - 1).astype(BF16)
    codes_f = (dosages - 1).astype(F32)
    new_f = (new_dosages - 1).astype(F32)
    trait_bf = traits.astype(BF16)
    parts = (
        jnp.sum(codes_f, axis=0),
        jnp.sum(codes_f * codes_f, axis=0),
        jnp.sum(new_f, axis=0),
        jnp.sum(new_f * new_f, axis=0),
        jnp.sum(trait_bf.astype(F32), axis=1),
    )
    sizes = [p.shape[0] for p in parts]
    slots = share_rows * 256
    sums = jnp.pad(jnp.concatenate(parts), (0, slots - sum(sizes))).reshape(share_rows, 256)
    first, second = codes[:, :half_width], codes[:, half_width:]
    over_rows = ((0,), (0,))
    gram_top = dot(first, codes, over_rows)
    gram_low = dot(second, second, over_rows)
    cross = dot(codes, trait_bf, ((0,), (1,)))
    wide = 3 * half_width
    payload = jnp.concatenate(
        [gram_top, gram_low, cross[:half_width], cross[half_width:]], axis=1
    ).reshape(samp, share_rows, wide + 2 * trait_count)
    payload = jnp.concatenate(
        [payload, jnp.broadcast_to(sums[None], (samp, share_rows, 256))], axis=2
    )
    chunk = jnp.sum(lax.all_to_all(payload, SAMP, 0, 0, tiled=True), axis=0)

    totals = chunk[:, wide + 2 * trait_count :].reshape(slots)
    pieces, at = [], 0
    for size in sizes:
        pieces.append(totals[at : at + size])
        at += size
    code_sum, code_sq, new_sum, new_sq, trait_sum = pieces
    mean, inv = column_stats(code_sum, code_sq, count)
    value_mean, slope, square = affine(code_sum, code_sq, mean, inv, count)

    start = lax.axis_index(SAMP) * share_rows

    def own(vector, offset):
        return lax.dynamic_slice(vector, (start + offset,), (share_rows,))[:, None]

    def centred(product, offset, column_from):
        sums_i, slope_i, value_i = (own(v, offset) for v in (code_sum, slope, value_mean))
        out = slope_i * slope[None, column_from:] * (
            product / count - (sums_i / count) * (code_sum[None, column_from:] / count)
        )
        out = out + value_i * value_mean[None, column_from:]
        row = start + offset + lax.broadcasted_iota(jnp.int32, out.shape, 0)
        column = column_from + lax.broadcasted_iota(jnp.int32, out.shape, 1)
        return jnp.where(row == column, 0.0, out)

    def centred_cross(product, offset):
        sums_i, slope_i, value_i = (own(v, offset) for v in (code_sum, slope, value_mean))
        trait_mean = trait_sum[None, :] / count
        return slope_i * (product / count - (sums_i / count) * trait_mean) + value_i * trait_mean

    rhs_rows = jnp.concatenate(
        [
            centred_cross(chunk[:, wide : wide + trait_count], 0),
            centred_cross(chunk[:, wide + trait_count : wide + 2 * trait_count], half_width),
        ],
        axis=1,
    )
    rhs_high = rounded(rhs_rows)
    own_rows = jnp.concatenate(
        [
            centred(chunk[:, :width], 0, 0),
            centred(chunk[:, width:wide], half_width, half_width),
            rhs_high,
            rhs_rows - rhs_high,
        ],
        axis=1,
    ).astype(BF16)
    every = lax.all_to_all(
        jnp.broadcast_to(own_rows[None], (samp, *own_rows.shape)), SAMP, 0, 0, tiled=True
    ).reshape(half_width, own_rows.shape[1])

    top_left, top_right = every[:, :half_width], every[:, half_width:width]
    low_right = every[:, width:wide]
    gram = jnp.concatenate(
        [
            jnp.concatenate([top_left, top_right], axis=1),
            jnp.concatenate([top_right.T, low_right], axis=1),
        ],
        axis=0,
    )
    bound = jnp.max(jnp.sum(jnp.abs(gram.astype(F32)), axis=0) + square)
    rhs_parts = every[:, wide:].reshape(half_width, 2, 2, trait_count)
    rhs_parts = rhs_parts.transpose(1, 3, 2, 0).reshape(2 * trait_count, width)

    def apply_gram(high, low, whole):
        out = dot(jnp.concatenate([high, low], axis=0), gram, ((1,), (0,)))
        return out[:trait_count] + out[trait_count:] + square[None, :] * whole

    high, low = rhs_parts[:trait_count], rhs_parts[trait_count:]
    rhs = high.astype(F32) + low.astype(F32)
    once = apply_gram(high, low, rhs)
    once_high = rounded(once)
    twice = apply_gram(once_high.astype(BF16), (once - once_high).astype(BF16), once)
    coefficients = chebyshev_coefficients(shrink, bound)

    row = lax.broadcasted_iota(jnp.int32, (columns, 3 * trait_count), 0)
    column = lax.broadcasted_iota(jnp.int32, (columns, 3 * trait_count), 1)
    side, in_side = row // (columns // cores), row % (columns // cores)
    place, in_place = in_side // (RIDGE * share), in_side % (RIDGE * share)
    ridge, in_share = in_place // share, in_place % share
    core = lax.rem(lax.axis_index("core") + 1 + side, cores)
    trait = (place * cores + core) * share + in_share
    mixing = jnp.zeros((columns, 3 * trait_count), F32)
    for power in range(3):
        for r in range(RIDGE):
            mixing = jnp.where(
                (ridge == r) & (column == trait + power * trait_count),
                coefficients[power][r],
                mixing,
            )
    weights = dot(
        mixing,
        jnp.concatenate([rhs, once, twice], axis=0),
        ((1,), (0,)),
        lax.Precision.HIGHEST,
    ).astype(BF16)

    standard = scaled(dosages, mean, inv)
    new_mean, new_inv = column_stats(new_sum, new_sq, count)
    fresh = scaled(new_dosages, new_mean, new_inv)

    half_columns = columns // cores
    along = ((1,), (1,))
    sent = dot(weights[:half_columns], standard, along).astype(BF16)
    kept = dot(weights[half_columns:], standard, along)
    arrived = lax.ppermute(sent, "core", [(0, 1), (1, 0)])
    paired = (kept + arrived.astype(F32)).astype(BF16).reshape(depth, RIDGE * share, rows)
    summed = lax.all_to_all(paired, "y", 0, 0, tiled=True)
    pred = jnp.sum(summed.astype(F32), axis=0).reshape(RIDGE, share, rows)

    own_traits = lax.dynamic_slice_in_dim(traits, lax.axis_index(BLK) * share, share, 0)
    residual = own_traits[None] - pred
    res_bf = lax.all_gather(
        residual.astype(BF16).reshape(RIDGE * share, rows), BLK, axis=0, tiled=True
    )
    raw_part = dot(res_bf, fresh, ((1,), (0,)))
    res_float = res_bf.astype(F32)
    squares = jnp.sum(res_float * res_float, axis=1).reshape(zs, 1, columns // zs)
    squares = jnp.pad(squares, ((0, 0), (0, 7), (0, fresh_width - columns // zs)))
    ends = jnp.concatenate([raw_part.reshape(zs, columns // zs, fresh_width), squares], axis=1)
    ends = jnp.sum(lax.all_to_all(ends, "z", 0, 0, tiled=True), axis=0)
    ends = lax.psum(ends, "x")
    raw, sum_sq = ends[: columns // zs], ends[columns // zs, : columns // zs]
    scores = raw / jnp.sqrt(count * (sum_sq / count + EPS))[:, None]
    scores = lax.all_to_all(
        jnp.broadcast_to(scores[None], (zs, *scores.shape)), "z", 0, 0, tiled=True
    )
    scores = scores.reshape(blk, RIDGE, share, fresh_width).transpose(1, 0, 2, 3)
    return residual, scores.reshape(RIDGE, trait_count, fresh_width)


def solution(mesh):
    samp, blk = FACTORS[mesh.shape["samp"]], FACTORS[mesh.shape["blk"]]
    grid = Mesh(mesh.devices.reshape(*samp, *blk), SAMP + BLK)
    return jax.shard_map(
        shards,
        mesh=grid,
        in_specs=(P(SAMP, BLK), P(SAMP, BLK), P(None, SAMP), P()),
        out_specs=(P(None, BLK, SAMP), P(None, None, BLK)),
        check_vma=False,
    )
```

time: 636 us -> 223 us (0.35)
  the two profiles are of different devices: /device:TPU:40 before, /device:TPU:8 now
where the time goes in v1:
time: 223 us; the launch traced here: 221 us
  waiting for transfers between devices  83.4 us (37%)
  starting transfers between devices  35.7 us (16%)
  blocking collectives  34.5 us (15%)
  local copies, waits for them, and re-layouts  25.3 us (11%)
  other arithmetic  20.5 us (9%)
  matrix products  20 us (9%)
    all_to_all x1, waiting for transfers between devices, shards(): chunk = jnp.sum(lax.all_to_all(payload, SAMP, 0, 0, tiled=True), axis=0)  30.3 us
    dot_general x9, matrix products, dot(): lax.dot_general(a, b, (contract, ((), ())), precision=precision, preferre...  20 us
    all_gather x1, blocking collectives, shards(): lax.all_gather(residual.astype(BF16).reshape(RIDGE * share, rows), BLK, a...  19.1 us
    all_to_all x1, waiting for transfers between devices, shards(): summed = lax.all_to_all(paired, 'y', 0, 0, tiled=True)  16.9 us
    psum x1, blocking collectives, shards(): ends = lax.psum(ends, 'x')  15.4 us
    all_to_all x1, waiting for transfers between devices, shards(): lax.all_to_all(jnp.broadcast_to(own_rows[None], (samp, *own_rows.shape)),...  14.7 us
    all_to_all x1, starting transfers between devices, shards(): chunk = jnp.sum(lax.all_to_all(payload, SAMP, 0, 0, tiled=True), axis=0)  13.3 us
    all_to_all x1, waiting for transfers between devices, shards(): ends = jnp.sum(lax.all_to_all(ends, 'z', 0, 0, tiled=True), axis=0)  11 us
  transfers between devices with their start and end apart: 6, of which 6 were waited for; matrix products, arithmetic and copies ran while one was open for 2% of the time, Pallas kernels for 0%

profile of v1, /device:TPU:8, one launch (start us, length us, event | category | flops | bytes accessed | tf_op | source)
XLA Modules:
  0.0 220.9 jit_solution(13262179598304185275)
XLA Ops:
  0.6 2.3 %add_convert_fusion = bf16[1536,512]{1,0:T(8,128)(2,1)S(1)} fusion(s32[1536,512]{1,0:T(8,128)} %param.4), kind=kLoop, calls=%fused_computation.3 | loop fusion | flops 1572864 | bytes 4718592 | tf_op jit(solution)/shard_map/convert_element_type | solution.py:83
  3.0 1.4 fusion.2
  4.4 1.1 fusion
  5.6 0.6 multiply_reduce_fusion
  6.6 2.1 fusion.119
  8.8 0.7 fusion.171
  9.8 1.3 constant_dynamic-update-slice_fusion.4
  11.1 1.3 constant_dynamic-update-slice_fusion.3
  12.4 1.3 constant_dynamic-update-slice_fusion.2
  13.6 1.3 constant_dynamic-update-slice_fusion.1
  14.9 1.3 constant_dynamic-update-slice_fusion
  16.2 0.7 pad.8
  16.9 1.4 maximum_bitcast_fusion
  18.3 1.1 pad_maximum_fusion
  19.4 13.3 %all-to-all-start = ((f32[32,8,1152]{2,1,0:T(8,128)}), f32[32,8,1152]{2,1,0:T(8,128)}, u32[]{:S(2)}, u32[]{:S(2)}) async-start(f32[32,8,1152]{2,1,0:T(8,128)} %pad_maximum_fusion), calls=%async_computation | async-start | bytes 2359296 | tf_op jit(solution)/shard_map/all_to_all | solution.py:109
  32.7 0.5 iota_add_fusion.2
  33.2 0.5 iota_add_fusion.1
  33.7 30.3 %all-to-all-done = f32[32,8,1152]{2,1,0:T(8,128)} async-done(((f32[32,8,1152]{2,1,0:T(8,128)}), f32[32,8,1152]{2,1,0:T(8,128)}, u32[]{:S(2)}, u32[]{:S(2)}) %all-to-all-start) | async-done | bytes 1179680 | tf_op jit(solution)/shard_map/all_to_all | solution.py:109
  64.0 2.0 reduce_sum.97
  66.0 0.8 slice_bitcast_fusion.1
  67.0 0.7 slice_multiply_fusion.4
  67.7 0.8 fusion.131
  68.5 0.6 copy-done.8
  69.1 0.8 fusion.138
  69.9 0.8 fusion.126
  70.8 0.9 broadcast_in_dim.108
  71.6 5.3 %all-to-all-start.1 = ((bf16[32,8,1024]{2,1,0:T(8,128)(2,1)}), bf16[32,8,1024]{2,1,0:T(8,128)(2,1)}, u32[]{:S(2)}, u32[]{:S(2)}) async-start(bf16[32,8,1024]{2,1,0:T(8,128)(2,1)} %broadcast_in_dim.108), calls=%async_computation.1 | async-start | bytes 1048576 | tf_op jit(solution)/shard_map/all_to_all | solution.py:157
  77.0 0.6 fusion.148
  77.6 0.6 iota_divide_fusion
  78.2 0.6 fusion.145
  78.7 14.7 %all-to-all-done.1 = bf16[32,8,1024]{2,1,0:T(8,128)(2,1)} async-done(((bf16[32,8,1024]{2,1,0:T(8,128)(2,1)}), bf16[32,8,1024]{2,1,0:T(8,128)(2,1)}, u32[]{:S(2)}, u32[]{:S(2)}) %all-to-all-start.1) | async-done | bytes 524320 | tf_op jit(solution)/shard_map/all_to_all | solution.py:157
  93.5 1.8 fusion.170
  95.3 1.7 concatenate.57
  96.9 1.7 copy.34
  98.6 1.2 abs_reduce_fusion
  99.8 0.6 reduce_sum.99
  100.4 1.4 fusion.150
  102.4 0.7 negate_multiply_fusion
  103.0 0.7 add_add_fusion.1
  103.7 0.7 fusion.176
  104.4 0.7 fusion.177
  105.1 0.7 fusion.175
  105.7 1.7 copy.28
  107.4 0.9 fusion.172
  108.5 1.3 fusion.111
  110.6 11.3 %convolution_convert_fusion.1 = bf16[320,512]{1,0:T(8,128)(2,1)S(1)} fusion(f32[64,512]{1,0:T(8,128)S(1)} %fusion.109, f32[64,512]{1,0:T(8,128)S(1)} %get-tuple-element.14, f32[64,512]{1,0:T(8,128)S(1)} %get-tuple-element.20, f32[]{:T(128)} %bitcast.18, f32[]{:T(128)} %bitcast.17, f32[]{:T(128)} %bitcast.16, f32[]{:T(128)} %bitcast.15, f32[]{:T(128)} %bitcast.14, ...), kind=kOutput, calls=%fused_computation.6 | convolution fusion | flops 383008768 | bytes 726720 | tf_op jit(solution)/shard_map/dot_general | solution.py:16
  121.8 0.7 convolution_convert_fusion
  122.5 1.9 collective-permute-start
  124.5 1.8 collective-permute-done
  126.3 1.5 add_convert_fusion.1
  127.8 2.0 reshape.255
  129.8 7.5 %all-to-all-start.2 = ((bf16[8,20,1536]{2,1,0:T(8,128)(2,1)}), bf16[8,20,1536]{2,1,0:T(8,128)(2,1)S(1)}, u32[]{:S(2)}, u32[]{:S(2)}) async-start(bf16[8,20,1536]{2,1,0:T(8,128)(2,1)} %reshape.255), calls=%async_computation.2 | async-start | bytes 1179648 | tf_op jit(solution)/shard_map/all_to_all | solution.py:217
  137.4 0.8 add_multiply_fusion.4
  138.1 16.9 %all-to-all-done.2 = bf16[8,20,1536]{2,1,0:T(8,128)(2,1)S(1)} async-done(((bf16[8,20,1536]{2,1,0:T(8,128)(2,1)}), bf16[8,20,1536]{2,1,0:T(8,128)(2,1)S(1)}, u32[]{:S(2)}, u32[]{:S(2)}) %all-to-all-start.2) | async-done | bytes 491552 | tf_op jit(solution)/shard_map/all_to_all | solution.py:217
  155.2 19.1 %all-gather = bf16[16,20,1536]{2,1,0:T(8,128)(2,1)S(1)} all-gather(bf16[1,20,1536]{2,1,0:T(8,128)(2,1)S(1)} %fusion.121), channel_id=1, replica_groups=mesh['x'=4,'z'=8,'y'=8,'core'=2] {'y','core'}, dimensions={0}, use_global_device_ids=true | all-gather | bytes 1044480 | tf_op jit(solution)/shard_map/all_gather | solution.py:222
  175.3 0.7 select_maximum_fusion
  176.0 4.2 %all-to-all-start.3 = ((f32[8,48,128]{2,1,0:T(8,128)}), f32[8,48,128]{2,1,0:T(8,128)S(1)}, u32[]{:S(2)}, u32[]{:S(2)}) async-start(f32[8,48,128]{2,1,0:T(8,128)} %select_maximum_fusion), calls=%async_computation.3 | async-start | bytes 393216 | tf_op jit(solution)/shard_map/all_to_all | solution.py:230
  180.3 11.0 %all-to-all-done.3 = f32[8,48,128]{2,1,0:T(8,128)S(1)} async-done(((f32[8,48,128]{2,1,0:T(8,128)}), f32[8,48,128]{2,1,0:T(8,128)S(1)}, u32[]{:S(2)}, u32[]{:S(2)}) %all-to-all-start.3) | async-done | bytes 196640 | tf_op jit(solution)/shard_map/all_to_all | solution.py:230
  191.3 15.4 %psum.7 = f32[48,128]{1,0:T(8,128)S(1)} all-reduce(f32[48,128]{1,0:T(8,128)S(1)} %reduce_sum.102), channel_id=1, replica_groups=mesh['x'=4,'z'=8,'y'=8,'core'=2] {'x'}, use_global_device_ids=true, to_apply=%region_11.12 | all-reduce | flops 6144 | bytes 49152 | tf_op jit(solution)/shard_map/psum | solution.py:231
  206.8 0.7 broadcast_in_dim.125
  207.4 3.4 %all-to-all-start.4 = ((f32[8,40,128]{2,1,0:T(8,128)}), f32[8,40,128]{2,1,0:T(8,128)S(1)}, u32[]{:S(2)}, u32[]{:S(2)}) async-start(f32[8,40,128]{2,1,0:T(8,128)} %broadcast_in_dim.125), calls=%async_computation.4 | async-start | bytes 327680 | tf_op jit(solution)/shard_map/all_to_all | solution.py:234
  210.8 0.7 broadcast_subtract_fusion
  211.5 8.7 %all-to-all-done.4 = f32[8,40,128]{2,1,0:T(8,128)S(1)} async-done(((f32[8,40,128]{2,1,0:T(8,128)}), f32[8,40,128]{2,1,0:T(8,128)S(1)}, u32[]{:S(2)}, u32[]{:S(2)}) %all-to-all-start.4) | async-done | bytes 163872 | tf_op jit(solution)/shard_map/all_to_all | solution.py:234
  220.2 0.7 copy.31
  (67 shorter events, 3.4 us)
Async XLA Ops:
  3.0 2.5 %copy-start.1 = (bf16[1536,512]{1,0:T(8,128)(2,1)}, bf16[1536,512]{1,0:T(8,128)(2,1)S(1)}, u32[]{:S(2)}) copy-start(bf16[1536,512]{1,0:T(8,128)(2,1)S(1)} %add_convert_fusion) | copy-start | bytes 4718596
  3.0 2.6 %copy-start = (s32[1536,512]{1,0:T(8,128)S(1)}, s32[1536,512]{1,0:T(8,128)}, u32[]{:S(2)}) copy-start(s32[1536,512]{1,0:T(8,128)} %param.4) | copy-start | bytes 9437188
  5.6 1.0 copy-start.4
  6.6 2.9 %copy-start.2 = (s32[1536,128]{1,0:T(8,128)S(1)}, s32[1536,128]{1,0:T(8,128)}, u32[]{:S(2)}) copy-start(s32[1536,128]{1,0:T(8,128)} %param.5) | copy-start | bytes 2359300
  19.4 44.6 %all-to-all-start = ((f32[32,8,1152]{2,1,0:T(8,128)}), f32[32,8,1152]{2,1,0:T(8,128)}, u32[]{:S(2)}, u32[]{:S(2)}) async-start(f32[32,8,1152]{2,1,0:T(8,128)} %pad_maximum_fusion), calls=%async_computation | async-start | bytes 2359296 | tf_op jit(solution)/shard_map/all_to_all | solution.py:109
  68.5 0.6 copy-start.8
  71.6 21.8 %all-to-all-start.1 = ((bf16[32,8,1024]{2,1,0:T(8,128)(2,1)}), bf16[32,8,1024]{2,1,0:T(8,128)(2,1)}, u32[]{:S(2)}, u32[]{:S(2)}) async-start(bf16[32,8,1024]{2,1,0:T(8,128)(2,1)} %broadcast_in_dim.108), calls=%async_computation.1 | async-start | bytes 1048576 | tf_op jit(solution)/shard_map/all_to_all | solution.py:157
  107.4 2.6 %copy-start.5 = (bf16[256,512]{1,0:T(8,128)(2,1)S(1)}, bf16[256,512]{1,0:T(8,128)(2,1)}, u32[]{:S(2)}) copy-start(bf16[256,512]{1,0:T(8,128)(2,1)} %concatenate.57) | copy-start | bytes 786436
  107.4 2.6 %copy-start.6 = (bf16[256,256]{0,1:T(8,128)(2,1)S(1)}, bf16[256,256]{0,1:T(8,128)(2,1)}, u32[]{:S(2)}) copy-start(bf16[256,256]{0,1:T(8,128)(2,1)} %copy.34) | copy-start | bytes 393220
  107.4 2.6 %copy-start.7 = (bf16[256,256]{1,0:T(8,128)(2,1)S(1)}, bf16[256,256]{1,0:T(8,128)(2,1)}, u32[]{:S(2)}) copy-start(bf16[256,256]{1,0:T(8,128)(2,1)} %get-tuple-element.17) | copy-start | bytes 393220
  109.8 0.7 copy-start.9
  109.9 0.7 copy-start.10
  109.9 0.7 copy-start.11
  109.9 0.7 copy-start.12
  109.9 0.7 copy-start.13
  109.9 0.7 copy-start.14
  122.5 3.8 %collective-permute-start = (bf16[160,1536]{1,0:T(8,128)(2,1)S(1)}, bf16[160,1536]{1,0:T(8,128)(2,1)S(1)}, u32[]{:S(2)}, u32[]{:S(2)}) collective-permute-start(bf16[160,1536]{1,0:T(8,128)(2,1)S(1)} %convolution_convert_fusion), channel_id=1, source_target_pairs={{0,1},{1,0},{2,3},{3,2},{4,5},{5,4},{6,7},{7,6},{8,9},{9,8},{10,11... | collective-permute-start | bytes 1474568 | tf_op jit(solution)/shard_map/ppermute | solution.py:215
  129.8 25.3 %all-to-all-start.2 = ((bf16[8,20,1536]{2,1,0:T(8,128)(2,1)}), bf16[8,20,1536]{2,1,0:T(8,128)(2,1)S(1)}, u32[]{:S(2)}, u32[]{:S(2)}) async-start(bf16[8,20,1536]{2,1,0:T(8,128)(2,1)} %reshape.255), calls=%async_computation.2 | async-start | bytes 1179648 | tf_op jit(solution)/shard_map/all_to_all | solution.py:217
  155.2 19.7 %copy-start.3 = (s32[1536,128]{1,0:T(8,128)S(1)}, s32[1536,128]{1,0:T(8,128)}, u32[]{:S(2)}) copy-start(s32[1536,128]{1,0:T(8,128)} %param.5) | copy-start | bytes 2359300
  176.0 15.2 %all-to-all-start.3 = ((f32[8,48,128]{2,1,0:T(8,128)}), f32[8,48,128]{2,1,0:T(8,128)S(1)}, u32[]{:S(2)}, u32[]{:S(2)}) async-start(f32[8,48,128]{2,1,0:T(8,128)} %select_maximum_fusion), calls=%async_computation.3 | async-start | bytes 393216 | tf_op jit(solution)/shard_map/all_to_all | solution.py:230
  207.4 12.7 %all-to-all-start.4 = ((f32[8,40,128]{2,1,0:T(8,128)}), f32[8,40,128]{2,1,0:T(8,128)S(1)}, u32[]{:S(2)}, u32[]{:S(2)}) async-start(f32[8,40,128]{2,1,0:T(8,128)} %broadcast_in_dim.125), calls=%async_computation.4 | async-start | bytes 327680 | tf_op jit(solution)/shard_map/all_to_all | solution.py:234

commit v2 on v1

v2 whole, which is shorter than its diff:
```python
import functools

import jax
import jax.numpy as jnp
from jax import lax
from jax.experimental import pallas as pl
from jax.experimental.pallas import tpu as pltpu
from jax.sharding import Mesh, PartitionSpec as P


RIDGE = 5
SAMP = ("x", "z")
BLK = ("y", "core")
FACTORS = {32: (4, 8), 16: (8, 2), 4: (2, 2)}
EPS = 1e-05
TILE = 128
SUMS = 3 * TILE
F32 = jnp.float32
BF16 = jnp.bfloat16
EXACT = lax.Precision.HIGHEST


def dot(a, b, contract, precision=None):
    return lax.dot_general(
        a, b, (contract, ((), ())), precision=precision, preferred_element_type=F32
    )


def rounded(values):
    return lax.reduce_precision(values, 8, 7)


def split(values):
    high = values.astype(BF16)
    return high, (values - high.astype(F32)).astype(BF16)


def gram_tiles(width, samp):
    at = 0
    for block_row in range(width // TILE):
        for block_column in range(block_row, width // TILE):
            for group in range(TILE // 8):
                yield block_row * TILE + 8 * group, block_column * TILE, at % samp, at // samp
                at += 1


def cross_tiles(trait_count, width, samp):
    at = 0
    for group in range(trait_count // 8):
        for block in range(width // TILE):
            yield 8 * group, block * TILE, at % samp, at // samp
            at += 1


def places(width, trait_count, samp):
    blocks = width // TILE
    gram = blocks * (blocks + 1) // 2 * (TILE // 8) // samp
    return gram, trait_count // 8 * blocks // samp


def products_kernel(samp, rows, dosages, new_dosages, traits, out, gram, cross, sums, new_sums, trait_sums):
    width, trait_count = dosages.shape[1], traits.shape[0]
    half = width // 2
    step = pl.program_id(0)

    @pl.when(step == 0)
    def _():
        for ref in (gram, cross, sums, new_sums, trait_sums):
            ref[...] = jnp.zeros_like(ref)

    codes_f = (dosages[...] - 1).astype(F32)
    codes = codes_f.astype(BF16)
    new_f = (new_dosages[...] - 1).astype(F32)
    trait_bf = traits[...].astype(BF16)
    ones = jnp.ones((8, codes.shape[0]), BF16)
    over_rows = ((0,), (0,))
    gram[:half, :] += dot(codes[:, :half], codes, over_rows)
    gram[half:, half:] += dot(codes[:, half:], codes[:, half:], over_rows)
    cross[...] += dot(trait_bf, codes, ((1,), (0,)))
    sums[:8] += dot(ones, codes, ((1,), (0,)))
    sums[8:] += dot(ones, (codes_f * codes_f).astype(BF16), ((1,), (0,)))
    new_sums[:8] += dot(ones, new_f.astype(BF16), ((1,), (0,)))
    new_sums[8:] += dot(ones, (new_f * new_f).astype(BF16), ((1,), (0,)))
    trait_sums[...] += dot(ones, trait_bf, ((1,), (1,)))

    @pl.when(step == pl.num_programs(0) - 1)
    def _():
        local = sums[:8]
        shift = 1.0 / (8.0 * rows)
        gram[...] = gram[...] - dot(local, local, over_rows, EXACT) * shift
        cross[...] = cross[...] - dot(trait_sums[...], local, over_rows, EXACT) * shift
        gram_places, cross_places = places(width, trait_count, samp)
        for row, column, owner, place in gram_tiles(width, samp):
            out[owner, :, place * TILE : (place + 1) * TILE] = gram[
                row : row + 8, column : column + TILE
            ].astype(BF16)
        for row, column, owner, place in cross_tiles(trait_count, width, samp):
            high, low = split(cross[row : row + 8, column : column + TILE])
            at = (gram_places + place) * TILE
            out[owner, :, at : at + TILE] = high
            at += cross_places * TILE
            out[owner, :, at : at + TILE] = low
        lines = []
        for block in range(4):
            line = [sums[0:1, block * TILE : (block + 1) * TILE], sums[8:9, block * TILE : (block + 1) * TILE]]
            if block == 0:
                line.append(new_sums[0:1])
            elif block == 1:
                line.append(new_sums[8:9])
            elif block == 2:
                spare = jnp.zeros((1, TILE - trait_count), F32)
                line.append(jnp.concatenate([trait_sums[0:1], spare], axis=1))
            else:
                line.append(jnp.zeros((1, TILE), F32))
            lines.append(jnp.concatenate(line, axis=1))
        values = jnp.concatenate(lines, axis=0)
        kept = rounded_in_kernel(values)
        packed = jnp.concatenate([kept, values - kept], axis=0).astype(BF16)
        at = (gram_places + 2 * cross_places) * TILE
        out[:, :, at:] = jnp.broadcast_to(packed[None], (samp, 8, SUMS))


def rounded_in_kernel(values):
    return values.astype(BF16).astype(F32)


def products(dosages, new_dosages, traits, samp):
    rows, width = dosages.shape
    fresh_width, trait_count = new_dosages.shape[1], traits.shape[0]
    gram_places, cross_places = places(width, trait_count, samp)
    lanes = (gram_places + 2 * cross_places) * TILE + SUMS
    step = min(512, rows)
    return pl.pallas_call(
        functools.partial(products_kernel, samp, rows),
        grid=(rows // step,),
        in_specs=[
            pl.BlockSpec((step, width), lambda i: (i, 0)),
            pl.BlockSpec((step, fresh_width), lambda i: (i, 0)),
            pl.BlockSpec((trait_count, step), lambda i: (0, i)),
        ],
        out_specs=pl.BlockSpec((samp, 8, lanes), lambda i: (0, 0, 0)),
        out_shape=jax.ShapeDtypeStruct((samp, 8, lanes), BF16),
        scratch_shapes=[
            pltpu.VMEM((width, width), F32),
            pltpu.VMEM((trait_count, width), F32),
            pltpu.VMEM((16, width), F32),
            pltpu.VMEM((16, fresh_width), F32),
            pltpu.VMEM((8, trait_count), F32),
        ],
        name="products",
    )(dosages, new_dosages, traits)


def owner_kernel(gram_lanes, cross_lanes, received, out, sums):
    samp = received.shape[0]
    values = received[:, :, gram_lanes + 2 * cross_lanes :].astype(F32)
    sums[...] = values[:, :4] + values[:, 4:]
    total = jnp.sum(received[:, :, : gram_lanes + 2 * cross_lanes].astype(F32), axis=0)
    cross = total[:, gram_lanes : gram_lanes + cross_lanes] + total[:, gram_lanes + cross_lanes :]
    high = rounded_in_kernel(cross)
    own = jnp.concatenate([total[:, :gram_lanes], high, cross - high], axis=1).astype(BF16)
    out[...] = jnp.broadcast_to(own[None], (samp, *own.shape))


def owner(received, gram_lanes, cross_lanes):
    lanes = gram_lanes + 2 * cross_lanes
    return pl.pallas_call(
        functools.partial(owner_kernel, gram_lanes, cross_lanes),
        out_shape=[
            jax.ShapeDtypeStruct((*received.shape[:2], lanes), BF16),
            jax.ShapeDtypeStruct((received.shape[0], 4, SUMS), F32),
        ],
        name="owner",
    )(received)


def column_stats(shifted_sum, shifted_sq, count):
    mean = (shifted_sum + count) / count
    var = (shifted_sq + 2.0 * shifted_sum + count) / count - mean * mean
    return mean, 1.0 / jnp.sqrt(var + EPS)


def scaled(codes, mean, inv):
    return ((codes.astype(F32) - mean) * inv).astype(BF16)


def affine(shifted_sum, shifted_sq, mean, inv, count):
    low, mid, high = (rounded((code - mean) * inv) for code in (0.0, 1.0, 2.0))
    n_low = (shifted_sq - shifted_sum) * 0.5
    n_high = (shifted_sq + shifted_sum) * 0.5
    n_mid = count - shifted_sq
    value_mean = (n_low * low + n_mid * mid + n_high * high) / count
    pairs = n_low * n_mid + n_mid * n_high + 4.0 * n_low * n_high
    slopes = (
        n_low * n_mid * (mid - low)
        + n_mid * n_high * (high - mid)
        + 2.0 * n_low * n_high * (high - low)
    )
    slope = jnp.where(pairs > 0.0, slopes / jnp.maximum(pairs, 1.0), inv)
    square = (n_low * low * low + n_mid * mid * mid + n_high * high * high) / count
    return value_mean, slope, square


def chebyshev_coefficients(lam, bound):
    centre = lam + bound / 2.0
    half = bound / 2.0
    sig = centre / half
    q0 = 1.0 / sig
    d0 = 1.0 / centre
    r1a, r1b = 1.0 - lam * d0, -d0
    q1 = 1.0 / (2.0 * sig - q0)
    step = 2.0 * q1 / half
    d1a, d1b = q1 * q0 * d0 + step * r1a, step * r1b
    r2a = r1a - lam * d1a
    r2b = r1b - d1a - lam * d1b
    r2c = -d1b
    q2 = 1.0 / (2.0 * sig - q1)
    step = 2.0 * q2 / half
    d2a, d2b, d2c = q2 * q1 * d1a + step * r2a, q2 * q1 * d1b + step * r2b, step * r2c
    return d0 + d1a + d2a, d1b + d2b, d2c


def ridge_kernel(count, depth, padded, core, lam, every, between, rhs_shift, slope, square, standard,
                 sent, kept, gram, cross, weights):
    samp = every.shape[0]
    width, trait_count = gram.shape[0], cross.shape[0]
    gram_places, cross_places = places(width, trait_count, samp)
    for row, column, owned, place in gram_tiles(width, samp):
        gram[row : row + 8, column : column + TILE] = every[
            owned, :, place * TILE : (place + 1) * TILE
        ].astype(F32)
    for block_row in range(width // TILE):
        for block_column in range(block_row + 1, width // TILE):
            gram[block_column * TILE : (block_column + 1) * TILE, block_row * TILE : (block_row + 1) * TILE] = gram[
                block_row * TILE : (block_row + 1) * TILE, block_column * TILE : (block_column + 1) * TILE
            ].T
    for row, column, owned, place in cross_tiles(trait_count, width, samp):
        at = (gram_places + place) * TILE
        low = at + cross_places * TILE
        cross[row : row + 8, column : column + TILE] = every[owned, :, at : at + TILE].astype(F32) + every[
            owned, :, low : low + TILE
        ].astype(F32)
    scale = slope[...]
    diagonal = square[...]
    matrix = gram[...] * (1.0 / count) + between[...]
    same = lax.broadcasted_iota(jnp.int32, matrix.shape, 0) == lax.broadcasted_iota(jnp.int32, matrix.shape, 1)
    matrix = jnp.where(same, 0.0, matrix)
    rhs = cross[...] * (1.0 / count) * scale + rhs_shift[...]

    def apply_gram(values):
        return dot(values * scale, matrix, ((1,), (0,)), EXACT) * scale + diagonal * values

    once = apply_gram(rhs)
    twice = apply_gram(once)
    eight = jnp.broadcast_to(scale, (8, width))
    column_sums = dot(eight, jnp.abs(matrix), ((1,), (0,)), EXACT)[0:1] * scale + diagonal
    bound = jnp.max(column_sums, axis=1, keepdims=True)
    for r in range(RIDGE):
        coefficients = chebyshev_coefficients(lam[r : r + 1, :], bound)
        a, b, c = (
            jnp.broadcast_to(jnp.concatenate([v] * (width // TILE), axis=1), (8, width))
            for v in coefficients
        )
        for y in range(depth):
            at, to = slice(8 * y, 8 * y + 8), 8 * (RIDGE * y + r)
            weights[to : to + 8] = a * rhs[at] + b * once[at] + c * twice[at]
    whole = weights[...].astype(BF16)

    def chosen(which):
        parts = []
        for y in range(depth):
            i = lax.broadcasted_iota(jnp.int32, (padded, whole.shape[0]), 0)
            j = lax.broadcasted_iota(jnp.int32, (padded, whole.shape[0]), 1)
            wanted = 8 * RIDGE * y + 2 * i - (i & 3) + 4 * which
            parts.append(((j == wanted) & (i < 4 * RIDGE)).astype(F32))
        select = jnp.concatenate(parts, axis=0).astype(BF16)
        return dot(select, whole, ((1,), (0,))).astype(BF16)

    mine = core[0]
    along = ((1,), (1,))
    sent[...] = dot(chosen(1 - mine), standard[...], along).astype(BF16)
    kept[...] = dot(chosen(mine), standard[...], along)


def ridge(core, lam, every, between, rhs_shift, slope, square, standard, count, depth, padded):
    rows, width = standard.shape
    trait_count = rhs_shift.shape[0]
    vmem = pl.BlockSpec(memory_space=pltpu.VMEM)
    return pl.pallas_call(
        functools.partial(ridge_kernel, count, depth, padded),
        in_specs=[pl.BlockSpec(memory_space=pltpu.SMEM)] + [vmem] * 7,
        out_specs=[vmem, vmem],
        out_shape=[
            jax.ShapeDtypeStruct((depth * padded, rows), BF16),
            jax.ShapeDtypeStruct((depth * padded, rows), F32),
        ],
        scratch_shapes=[
            pltpu.VMEM((width, width), F32),
            pltpu.VMEM((trait_count, width), F32),
            pltpu.VMEM((RIDGE * trait_count, width), F32),
        ],
        name="ridge",
    )(core, lam, every, between, rhs_shift, slope, square, standard)


def from_sums(sums, dosages, new_dosages, trait_count, count):
    (rows, width), samp = dosages.shape, sums.shape[0]
    code_sums = sums[:, :, :TILE].reshape(samp, width)
    trait_sums = sums[:, 2, 2 * TILE : 2 * TILE + trait_count]
    totals = jnp.sum(sums, axis=0)
    code_sum, code_sq = totals[:, :TILE].reshape(width), totals[:, TILE : 2 * TILE].reshape(width)
    new_sum, new_sq = totals[0, 2 * TILE :], totals[1, 2 * TILE :]
    trait_sum = totals[2, 2 * TILE : 2 * TILE + trait_count]
    mean, inv = column_stats(code_sum, code_sq, count)
    value_mean, slope, square = affine(code_sum, code_sq, mean, inv, count)
    new_mean, new_inv = column_stats(new_sum, new_sq, count)
    standard = scaled(dosages, mean, inv)
    fresh = scaled(new_dosages, new_mean, new_inv)
    code_shift = code_sums / rows - code_sum / count
    trait_shift = trait_sums / rows - trait_sum / count
    over_parts = ((0,), (0,))
    between = dot(code_shift, code_shift, over_parts, EXACT) * (1.0 / samp)
    rhs_shift = dot(trait_shift, code_shift, over_parts, EXACT) * (slope[None] * (1.0 / samp))
    rhs_shift = rhs_shift + (trait_sum / count)[:, None] * value_mean[None]
    return standard, fresh, between, rhs_shift, slope, square


def shards(dosages, new_dosages, traits, shrink):
    rows, width = dosages.shape
    fresh_width = new_dosages.shape[1]
    trait_count = traits.shape[0]
    samp, blk = lax.axis_size(SAMP), lax.axis_size(BLK)
    depth, xs, zs = lax.axis_size("y"), lax.axis_size("x"), lax.axis_size("z")
    count = float(rows * samp)
    share = trait_count // blk
    used = RIDGE * share
    padded = (used // 8 + 1) * 8
    gram_places, cross_places = places(width, trait_count, samp)

    payload = products(dosages, new_dosages, traits, samp)
    received = lax.all_to_all(payload, SAMP, 0, 0, tiled=True)
    own_rows, sums = owner(received, gram_places * TILE, cross_places * TILE)
    every = lax.all_to_all(own_rows, SAMP, 0, 0, tiled=True)
    prepared = from_sums(sums, dosages, new_dosages, trait_count, count)
    standard, fresh, between, rhs_shift, slope, square = prepared

    core = lax.axis_index("core").astype(jnp.int32).reshape(1)
    lam = jnp.broadcast_to(jnp.pad(shrink, (0, 3), constant_values=1.0)[:, None], (8, TILE))
    sent, kept = ridge(
        core, lam, every, between, rhs_shift, slope[None], square[None], standard, count, depth, padded
    )

    arrived = lax.ppermute(sent, "core", [(0, 1), (1, 0)])
    paired = (kept + arrived.astype(F32)).astype(BF16).reshape(depth, padded, rows)
    summed = lax.all_to_all(paired, "y", 0, 0, tiled=True)
    pred = jnp.sum(summed.astype(F32), axis=0)[:used].reshape(RIDGE, share, rows)

    own_traits = lax.dynamic_slice_in_dim(traits, lax.axis_index(BLK) * share, share, 0)
    residual = own_traits[None] - pred
    res_bf = lax.all_gather(residual.astype(BF16).reshape(1, used, rows), BLK, axis=0, tiled=True)
    res_bf = res_bf.reshape(blk * used, rows)
    raw_part = dot(res_bf, fresh, ((1,), (0,))).reshape(blk, used, fresh_width)
    res_float = res_bf.astype(F32)
    squares = jnp.sum(res_float * res_float, axis=1).reshape(blk, 1, used)
    squares = jnp.pad(squares, ((0, 0), (0, padded - used - 1), (0, fresh_width - used)))
    ends = jnp.concatenate([raw_part, squares], axis=1)
    ends = lax.all_to_all(ends.reshape(zs, blk // zs * padded, fresh_width), "z", 0, 0, tiled=True)
    ends = jnp.sum(ends, axis=0)
    ends = lax.all_to_all(jnp.broadcast_to(ends[None], (xs, *ends.shape)), "x", 0, 0, tiled=True)
    ends = jnp.sum(ends, axis=0).reshape(blk // zs, padded, fresh_width)
    sum_sq = ends[:, used, :used]
    scores = ends[:, :used] / jnp.sqrt(count * (sum_sq / count + EPS))[:, :, None]
    scores = scores.reshape(blk // zs * used, fresh_width)
    scores = lax.all_to_all(
        jnp.broadcast_to(scores[None], (zs, *scores.shape)), "z", 0, 0, tiled=True
    )
    scores = scores.reshape(blk, RIDGE, share, fresh_width).transpose(1, 0, 2, 3)
    return residual, scores.reshape(RIDGE, trait_count, fresh_width)


def solution(mesh):
    samp, blk = FACTORS[mesh.shape["samp"]], FACTORS[mesh.shape["blk"]]
    grid = Mesh(mesh.devices.reshape(*samp, *blk), SAMP + BLK)
    return jax.shard_map(
        shards,
        mesh=grid,
        in_specs=(P(SAMP, BLK), P(SAMP, BLK), P(None, SAMP), P()),
        out_specs=(P(None, BLK, SAMP), P(None, None, BLK)),
        check_vma=False,
    )
```

time: 223 us -> 164 us (0.74)
  local copies, waits for them, and re-layouts: 25.3 us -> 3.61 us
  waiting for transfers between devices: 83.4 us -> 63.4 us
  matrix products: 20 us -> 3.46 us
  Pallas kernels: 0 us -> 14.6 us
  other arithmetic: 20.5 us -> 8.42 us
    all_to_all x3, waiting for transfers between devices: 56 us -> 35.7 us  [the longest x1 20.1 us: shards(): received = lax.all_to_all(payload, SAMP, 0, 0, tiled=True)]
    dot_general x9 -> x3, matrix products: 20 us -> 3.46 us  [dot(): lax.dot_general(a, b, (contract, ((), ())), precision=precision, preferre...]
    psum x1 -> x0, blocking collectives: 15.4 us -> none  [shards(): ends = lax.psum(ends, 'x')]
    all_to_all x0 -> x1, blocking collectives: none -> 15 us  [shards(): lax.all_to_all(ends.reshape(zs, blk // zs * padded, fresh_width), 'z', 0,...]
    pallas_call x0 -> x3, Pallas kernels: none -> 14.6 us  [the longest x1 6.54 us: ridge(): pl.pallas_call(functools.partial(ridge_kernel, count, depth, padded), in_...]
    unnamed x42 -> x6, local copies, waits for them, and re-layouts: 9.3 us -> 0.02 us
    slice x11 -> x0, local copies, waits for them, and re-layouts: 7.26 us -> none  [the longest x3 2 us: shards(): coefficients[power][r]]
    add x7 -> x0, other arithmetic: 3.18 us -> none  [the longest x2 1.04 us: centred(): row = start + offset + lax.broadcasted_iota(jnp.int32, out.shape, 0)]
  transfers between devices with their start and end apart: 6 -> 6, of which waited for: 6 -> 6; matrix products, arithmetic and copies ran while one was open for 2% -> 4% of each run, Pallas kernels for 0% -> 0%
where the time goes in v2:
time: 164 us; the launch traced here: 163 us
  waiting for transfers between devices  63.4 us (39%)
  starting transfers between devices  34.7 us (21%)
  blocking collectives  34.1 us (21%)
  Pallas kernels  14.6 us (9%)
  other arithmetic  8.42 us (5%)
  local copies, waits for them, and re-layouts  3.61 us (2%)
  matrix products  3.46 us (2%)
    all_to_all x1, waiting for transfers between devices, shards(): received = lax.all_to_all(payload, SAMP, 0, 0, tiled=True)  20.1 us
    all_gather x1, blocking collectives, shards(): lax.all_gather(residual.astype(BF16).reshape(1, used, rows), BLK, axis=0,...  19.1 us
    all_to_all x1, waiting for transfers between devices, shards(): summed = lax.all_to_all(paired, 'y', 0, 0, tiled=True)  16.8 us
    all_to_all x1, blocking collectives, shards(): lax.all_to_all(ends.reshape(zs, blk // zs * padded, fresh_width), 'z', 0,...  15 us
    all_to_all x1, starting transfers between devices, shards(): received = lax.all_to_all(payload, SAMP, 0, 0, tiled=True)  13.3 us
    all_to_all x1, waiting for transfers between devices, shards(): every = lax.all_to_all(own_rows, SAMP, 0, 0, tiled=True)  9.92 us
    all_to_all x1, waiting for transfers between devices, shards(): lax.all_to_all(jnp.broadcast_to(scores[None], (zs, *scores.shape)), 'z',...  8.67 us
    all_to_all x1, starting transfers between devices, shards(): summed = lax.all_to_all(paired, 'y', 0, 0, tiled=True)  7.55 us
  transfers between devices with their start and end apart: 6, of which 6 were waited for; matrix products, arithmetic and copies ran while one was open for 4% of the time, Pallas kernels for 0%

profile of v2, /device:TPU:8, one launch (start us, length us, event | category | flops | bytes accessed | tf_op | source)
XLA Modules:
  0.0 163.1 jit_solution(13220030674922442189)
XLA Ops:
  0.6 0.0 copy-start.2
  0.6 6.0 %products.1 = bf16[32,8,1280]{2,1,0:T(8,128)(2,1)} custom-call(s32[1536,512]{1,0:T(8,128)} %dosages.1, s32[1536,128]{1,0:T(8,128)} %new_dosages.1, f32[64,1536]{1,0:T(8,128)} %traits.1), custom_call_target="tpu_custom_call" | custom-call | tf_op jit(solution)/shard_map/products/pallas_call | solution.py:133
  6.7 13.3 %all-to-all-start = ((bf16[32,8,1280]{2,1,0:T(8,128)(2,1)}), bf16[32,8,1280]{2,1,0:T(8,128)(2,1)}, u32[]{:S(2)}, u32[]{:S(2)}) async-start(bf16[32,8,1280]{2,1,0:T(8,128)(2,1)} %products.1), calls=%async_computation | async-start | bytes 1310720 | tf_op jit(solution)/shard_map/all_to_all | solution.py:341
  20.0 0.0 copy-done.2
  20.0 0.0 copy-start
  20.0 20.1 %all-to-all-done.received = bf16[32,8,1280]{2,1,0:T(8,128)(2,1)} async-done(((bf16[32,8,1280]{2,1,0:T(8,128)(2,1)}), bf16[32,8,1280]{2,1,0:T(8,128)(2,1)}, u32[]{:S(2)}, u32[]{:S(2)}) %all-to-all-start) | async-done | bytes 655392 | tf_op jit(solution)/shard_map/all_to_all | solution.py:341
  40.1 2.0 %owner.1 = (bf16[32,8,896]{2,1,0:T(8,128)(2,1)}, f32[32,4,384]{2,1,0:T(4,128)}) custom-call(bf16[32,8,1280]{2,1,0:T(8,128)(2,1)} %all-to-all-done.received), custom_call_target="tpu_custom_call" | custom-call | tf_op jit(solution)/shard_map/owner/pallas_call | solution.py:167
  42.1 1.0 reduce_sum.45
  43.1 0.9 multiply_subtract_fusion
  44.0 0.9 multiply_subtract_fusion.1
  44.9 5.3 %all-to-all-start.1 = ((bf16[32,8,896]{2,1,0:T(8,128)(2,1)}), bf16[32,8,896]{2,1,0:T(8,128)(2,1)}, u32[]{:S(2)}, u32[]{:S(2)}) async-start(bf16[32,8,896]{2,1,0:T(8,128)(2,1)} %get-tuple-element.6), calls=%async_computation.1 | async-start | bytes 917504 | tf_op jit(solution)/shard_map/all_to_all | solution.py:343
  50.1 1.0 fusion.rhs_shift
  51.1 0.6 fusion.22
  51.7 2.0 %convolution_multiply_fusion.between = f32[512,512]{1,0:T(8,128)} fusion(f32[4,8,4,128]{3,2,1,0:T(4,128)S(1)} %bitcast.89), kind=kOutput, calls=%fused_computation.2 | convolution fusion | flops 100925440 | bytes 1114112 | tf_op jit(solution)/shard_map/dot_general | solution.py:24
  53.7 0.0 copy-done
  53.7 1.6 multiply_convert_fusion.standard
  55.3 9.9 %all-to-all-done.1.every = bf16[32,8,896]{2,1,0:T(8,128)(2,1)} async-done(((bf16[32,8,896]{2,1,0:T(8,128)(2,1)}), bf16[32,8,896]{2,1,0:T(8,128)(2,1)}, u32[]{:S(2)}, u32[]{:S(2)}) %all-to-all-start.1) | async-done | bytes 458784 | tf_op jit(solution)/shard_map/all_to_all | solution.py:343
  65.2 0.7 broadcast_in_dim.8.lam
  65.9 6.5 %ridge.1 = (bf16[192,1536]{1,0:T(8,128)(2,1)}, f32[192,1536]{1,0:T(8,128)}) custom-call(s32[1]{0:T(128)} %bitcast.core, f32[8,128]{1,0:T(8,128)} %broadcast_in_dim.8.lam, bf16[32,8,896]{2,1,0:T(8,128)(2,1)} %all-to-all-done.1.every, f32[512,512]{1,0:T(8,128)} %convolution_multiply_fusion.between, f32[64,512]{1,0:T(8,128)} %fusion.rhs_shift, ...), custom_call_target="tpu_custom_call" | custom-call | tf_op jit(solution)/shard_map/ridge/pallas_call | solution.py:289
  72.4 1.9 %collective-permute-start = (bf16[192,1536]{1,0:T(8,128)(2,1)}, bf16[192,1536]{1,0:T(8,128)(2,1)S(1)}, u32[]{:S(2)}, u32[]{:S(2)}) collective-permute-start(bf16[192,1536]{1,0:T(8,128)(2,1)} %get-tuple-element.9), channel_id=1, source_target_pairs={{0,1},{1,0},{2,3},{3,2},{4,5},{5,4},{6,7},{7,6},{8,9},{9,8},{10,11... | collective-permute-start | bytes 1769480 | tf_op jit(solution)/shard_map/ppermute | solution.py:353
  74.4 2.2 %collective-permute-done = bf16[192,1536]{1,0:T(8,128)(2,1)S(1)} collective-permute-done((bf16[192,1536]{1,0:T(8,128)(2,1)}, bf16[192,1536]{1,0:T(8,128)(2,1)S(1)}, u32[]{:S(2)}, u32[]{:S(2)}) %collective-permute-start) | collective-permute-done | bytes 589856 | tf_op jit(solution)/shard_map/ppermute | solution.py:353
  76.5 2.2 %add_convert_fusion = bf16[192,1536]{1,0:T(8,128)(2,1)} fusion(f32[192,1536]{1,0:T(8,128)} %get-tuple-element.8, bf16[192,1536]{1,0:T(8,128)(2,1)S(1)} %collective-permute-done), kind=kLoop, calls=%fused_computation.4 | loop fusion | flops 884736 | bytes 2359296 | tf_op jit(solution)/shard_map/convert_element_type | solution.py:354
  78.7 7.6 %all-to-all-start.2 = ((bf16[8,24,1536]{2,1,0:T(8,128)(2,1)}), bf16[8,24,1536]{2,1,0:T(8,128)(2,1)S(1)}, u32[]{:S(2)}, u32[]{:S(2)}) async-start(bf16[8,24,1536]{2,1,0:T(8,128)(2,1)} %bitcast.7), calls=%async_computation.2 | async-start | bytes 1179648 | tf_op jit(solution)/shard_map/all_to_all | solution.py:355
  86.3 0.8 constant_dynamic-slice_fusion
  87.2 16.8 %all-to-all-done.2 = bf16[8,24,1536]{2,1,0:T(8,128)(2,1)S(1)} async-done(((bf16[8,24,1536]{2,1,0:T(8,128)(2,1)}), bf16[8,24,1536]{2,1,0:T(8,128)(2,1)S(1)}, u32[]{:S(2)}, u32[]{:S(2)}) %all-to-all-start.2) | async-done | bytes 589856 | tf_op jit(solution)/shard_map/all_to_all | solution.py:355
  104.0 0.1 convert_reduce_fusion
  104.1 0.0 copy-start.1
  104.2 19.1 %all-gather.1 = bf16[16,20,1536]{2,1,0:T(8,128)(2,1)S(1)} all-gather(bf16[1,20,1536]{2,1,0:T(8,128)(2,1)S(1)} %get-tuple-element.12), channel_id=2, replica_groups=mesh['x'=4,'z'=8,'y'=8,'core'=2] {'y','core'}, dimensions={0}, use_global_device_ids=true | all-gather | bytes 1044480 | tf_op jit(solution)/shard_map/all_gather | solution.py:360
  123.3 0.3 multiply_reduce_fusion
  123.6 0.0 copy-done.1
  123.6 0.5 fusion.2
  124.1 15.0 %all_to_all.30 = f32[8,48,128]{2,1,0:T(8,128)S(1)} all-to-all(f32[8,48,128]{2,1,0:T(8,128)S(1)} %bitcast.86), channel_id=1, replica_groups=mesh['x'=4,'z'=8,'y'=8,'core'=2] {'z'}, dimensions={0} | all-to-all | bytes 393216 | tf_op jit(solution)/shard_map/all_to_all | solution.py:367
  139.1 0.6 broadcast_in_dim.9
  139.8 3.3 %all-to-all-start.4 = ((f32[4,48,128]{2,1,0:T(8,128)}), f32[4,48,128]{2,1,0:T(8,128)S(1)}, u32[]{:S(2)}, u32[]{:S(2)}) async-start(f32[4,48,128]{2,1,0:T(8,128)} %broadcast_in_dim.9), calls=%async_computation.4 | async-start | bytes 196608 | tf_op jit(solution)/shard_map/all_to_all | solution.py:369
  143.1 5.7 %all-to-all-done.4 = f32[4,48,128]{2,1,0:T(8,128)S(1)} async-done(((f32[4,48,128]{2,1,0:T(8,128)}), f32[4,48,128]{2,1,0:T(8,128)S(1)}, u32[]{:S(2)}, u32[]{:S(2)}) %all-to-all-start.4) | async-done | bytes 98336 | tf_op jit(solution)/shard_map/all_to_all | solution.py:369
  148.9 0.1 slice_divide_fusion
  149.0 0.7 broadcast_in_dim.11
  149.7 3.4 %all-to-all-start.5 = ((f32[8,40,128]{2,1,0:T(8,128)}), f32[8,40,128]{2,1,0:T(8,128)S(1)}, u32[]{:S(2)}, u32[]{:S(2)}) async-start(f32[8,40,128]{2,1,0:T(8,128)} %broadcast_in_dim.11), calls=%async_computation.5 | async-start | bytes 327680 | tf_op jit(solution)/shard_map/all_to_all | solution.py:374
  153.1 0.7 broadcast_subtract_fusion
  153.7 8.7 %all-to-all-done.5 = f32[8,40,128]{2,1,0:T(8,128)S(1)} async-done(((f32[8,40,128]{2,1,0:T(8,128)}), f32[8,40,128]{2,1,0:T(8,128)S(1)}, u32[]{:S(2)}, u32[]{:S(2)}) %all-to-all-start.5) | async-done | bytes 163872 | tf_op jit(solution)/shard_map/all_to_all | solution.py:374
  162.4 0.7 copy.9
  (15 shorter events, 0.2 us)
Async XLA Ops:
  0.6 19.3 %copy-start.2 = (f32[5]{0:T(128)S(1)}, f32[5]{0:T(128)}, u32[]{:S(2)}) copy-start(f32[5]{0:T(128)} %param.7) | copy-start | bytes 64
  6.7 33.4 %all-to-all-start = ((bf16[32,8,1280]{2,1,0:T(8,128)(2,1)}), bf16[32,8,1280]{2,1,0:T(8,128)(2,1)}, u32[]{:S(2)}, u32[]{:S(2)}) async-start(bf16[32,8,1280]{2,1,0:T(8,128)(2,1)} %products.1), calls=%async_computation | async-start | bytes 1310720 | tf_op jit(solution)/shard_map/all_to_all | solution.py:341
  20.0 33.7 %copy-start = (s32[1536,512]{1,0:T(8,128)S(1)}, s32[1536,512]{1,0:T(8,128)}, u32[]{:S(2)}) copy-start(s32[1536,512]{1,0:T(8,128)} %dosages.1) | copy-start | bytes 9437188
  44.9 20.4 %all-to-all-start.1 = ((bf16[32,8,896]{2,1,0:T(8,128)(2,1)}), bf16[32,8,896]{2,1,0:T(8,128)(2,1)}, u32[]{:S(2)}, u32[]{:S(2)}) async-start(bf16[32,8,896]{2,1,0:T(8,128)(2,1)} %get-tuple-element.6), calls=%async_computation.1 | async-start | bytes 917504 | tf_op jit(solution)/shard_map/all_to_all | solution.py:343
  72.4 4.1 %collective-permute-start = (bf16[192,1536]{1,0:T(8,128)(2,1)}, bf16[192,1536]{1,0:T(8,128)(2,1)S(1)}, u32[]{:S(2)}, u32[]{:S(2)}) collective-permute-start(bf16[192,1536]{1,0:T(8,128)(2,1)} %get-tuple-element.9), channel_id=1, source_target_pairs={{0,1},{1,0},{2,3},{3,2},{4,5},{5,4},{6,7},{7,6},{8,9},{9,8},{10,11... | collective-permute-start | bytes 1769480 | tf_op jit(solution)/shard_map/ppermute | solution.py:353
  78.7 25.3 %all-to-all-start.2 = ((bf16[8,24,1536]{2,1,0:T(8,128)(2,1)}), bf16[8,24,1536]{2,1,0:T(8,128)(2,1)S(1)}, u32[]{:S(2)}, u32[]{:S(2)}) async-start(bf16[8,24,1536]{2,1,0:T(8,128)(2,1)} %bitcast.7), calls=%async_computation.2 | async-start | bytes 1179648 | tf_op jit(solution)/shard_map/all_to_all | solution.py:355
  104.1 19.5 %copy-start.1 = (s32[1536,128]{1,0:T(8,128)S(1)}, s32[1536,128]{1,0:T(8,128)}, u32[]{:S(2)}) copy-start(s32[1536,128]{1,0:T(8,128)} %new_dosages.1) | copy-start | bytes 2359300
  139.8 9.1 %all-to-all-start.4 = ((f32[4,48,128]{2,1,0:T(8,128)}), f32[4,48,128]{2,1,0:T(8,128)S(1)}, u32[]{:S(2)}, u32[]{:S(2)}) async-start(f32[4,48,128]{2,1,0:T(8,128)} %broadcast_in_dim.9), calls=%async_computation.4 | async-start | bytes 196608 | tf_op jit(solution)/shard_map/all_to_all | solution.py:369
  149.7 12.7 %all-to-all-start.5 = ((f32[8,40,128]{2,1,0:T(8,128)}), f32[8,40,128]{2,1,0:T(8,128)S(1)}, u32[]{:S(2)}, u32[]{:S(2)}) async-start(f32[8,40,128]{2,1,0:T(8,128)} %broadcast_in_dim.11), calls=%async_computation.5 | async-start | bytes 327680 | tf_op jit(solution)/shard_map/all_to_all | solution.py:374

commit v3 on v2

--- a/solution.py
+++ b/solution.py
@@ -17,6 +17,7 @@
 SUMS = 3 * TILE
 F32 = jnp.float32
 BF16 = jnp.bfloat16
+LIMIT = 30 << 20
 EXACT = lax.Precision.HIGHEST
 
 
@@ -170,6 +171,7 @@
             jax.ShapeDtypeStruct((*received.shape[:2], lanes), BF16),
             jax.ShapeDtypeStruct((received.shape[0], 4, SUMS), F32),
         ],
+        compiler_params=pltpu.CompilerParams(vmem_limit_bytes=LIMIT),
         name="owner",
     )(received)
 
@@ -220,8 +222,8 @@
     return d0 + d1a + d2a, d1b + d2b, d2c
 
 
-def ridge_kernel(count, depth, padded, core, lam, every, between, rhs_shift, slope, square, standard,
-                 sent, kept, gram, cross, weights):
+def ridge_kernel(count, depth, lam, core, every, between, rhs_shift, slope, square, standard,
+                 sent, own, gram, cross, weights, swapped):
     samp = every.shape[0]
     width, trait_count = gram.shape[0], cross.shape[0]
     gram_places, cross_places = places(width, trait_count, samp)
@@ -255,52 +257,105 @@
     eight = jnp.broadcast_to(scale, (8, width))
     column_sums = dot(eight, jnp.abs(matrix), ((1,), (0,)), EXACT)[0:1] * scale + diagonal
     bound = jnp.max(column_sums, axis=1, keepdims=True)
+    powers = [(v, swapped_tiles(v)) for v in (rhs, once, twice)]
     for r in range(RIDGE):
-        coefficients = chebyshev_coefficients(lam[r : r + 1, :], bound)
-        a, b, c = (
-            jnp.broadcast_to(jnp.concatenate([v] * (width // TILE), axis=1), (8, width))
-            for v in coefficients
-        )
+        coefficients = [
+            jnp.broadcast_to(v, (8, width))
+            for v in chebyshev_coefficients(jnp.full((1, 1), lam[r], F32), bound)
+        ]
         for y in range(depth):
             at, to = slice(8 * y, 8 * y + 8), 8 * (RIDGE * y + r)
-            weights[to : to + 8] = a * rhs[at] + b * once[at] + c * twice[at]
-    whole = weights[...].astype(BF16)
-
-    def chosen(which):
-        parts = []
-        for y in range(depth):
-            i = lax.broadcasted_iota(jnp.int32, (padded, whole.shape[0]), 0)
-            j = lax.broadcasted_iota(jnp.int32, (padded, whole.shape[0]), 1)
-            wanted = 8 * RIDGE * y + 2 * i - (i & 3) + 4 * which
-            parts.append(((j == wanted) & (i < 4 * RIDGE)).astype(F32))
-        select = jnp.concatenate(parts, axis=0).astype(BF16)
-        return dot(select, whole, ((1,), (0,))).astype(BF16)
-
+            for which, ref in enumerate((weights, swapped)):
+                ref[to : to + 8] = sum(c * p[which][at] for c, p in zip(coefficients, powers))
+    side = (lax.broadcasted_iota(jnp.int32, weights.shape, 0) >> 2) & 1
     mine = core[0]
+    both = weights[...], swapped[...]
+    own[...] = jnp.where(side == mine, *both).astype(BF16)
+    sent[...] = halves(jnp.where(side == 1 - mine, *both).astype(BF16), standard)
+
+
+def swapped_tiles(values):
+    tiles = [jnp.roll(values[at : at + 8], 4, axis=0) for at in range(0, values.shape[0], 8)]
+    return jnp.concatenate(tiles, axis=0)
+
+
+def halves(weights, standard):
+    half = standard.shape[0] // 2
     along = ((1,), (1,))
-    sent[...] = dot(chosen(1 - mine), standard[...], along).astype(BF16)
-    kept[...] = dot(chosen(mine), standard[...], along)
-
-
-def ridge(core, lam, every, between, rhs_shift, slope, square, standard, count, depth, padded):
+    first = dot(weights, standard[:half], along)
+    second = dot(weights, standard[half:], along)
+    low = (lax.broadcasted_iota(jnp.int32, first.shape, 0) & 4) == 0
+    return jnp.where(low, first, second).astype(BF16)
+
+
+def ridge(lam, core, every, between, rhs_shift, slope, square, standard, count, depth):
     rows, width = standard.shape
     trait_count = rhs_shift.shape[0]
-    vmem = pl.BlockSpec(memory_space=pltpu.VMEM)
+    vmem, smem = pl.BlockSpec(memory_space=pltpu.VMEM), pl.BlockSpec(memory_space=pltpu.SMEM)
     return pl.pallas_call(
-        functools.partial(ridge_kernel, count, depth, padded),
-        in_specs=[pl.BlockSpec(memory_space=pltpu.SMEM)] + [vmem] * 7,
+        functools.partial(ridge_kernel, count, depth),
+        in_specs=[smem] * 2 + [vmem] * 6,
         out_specs=[vmem, vmem],
         out_shape=[
-            jax.ShapeDtypeStruct((depth * padded, rows), BF16),
-            jax.ShapeDtypeStruct((depth * padded, rows), F32),
+            jax.ShapeDtypeStruct((RIDGE * trait_count, rows // 2), BF16),
+            jax.ShapeDtypeStruct((RIDGE * trait_count, width), BF16),
         ],
         scratch_shapes=[
             pltpu.VMEM((width, width), F32),
             pltpu.VMEM((trait_count, width), F32),
             pltpu.VMEM((RIDGE * trait_count, width), F32),
-        ],
+            pltpu.VMEM((RIDGE * trait_count, width), F32),
+        ],
+        compiler_params=pltpu.CompilerParams(vmem_limit_bytes=LIMIT),
         name="ridge",
-    )(core, lam, every, between, rhs_shift, slope, square, standard)
+    )(lam, core, every, between, rhs_shift, slope, square, standard)
+
+
+def kept_kernel(weights, standard, out):
+    out[...] = halves(weights[...], standard)
+
+
+def kept_rows(weights, standard):
+    vmem = pl.BlockSpec(memory_space=pltpu.VMEM)
+    return pl.pallas_call(
+        kept_kernel,
+        in_specs=[vmem, vmem],
+        out_specs=vmem,
+        out_shape=jax.ShapeDtypeStruct((weights.shape[0], standard.shape[0] // 2), BF16),
+        compiler_params=pltpu.CompilerParams(vmem_limit_bytes=LIMIT),
+        name="kept",
+    )(weights, standard)
+
+
+def residual_kernel(summed, own_traits, out, out_bf, flat):
+    pred = jnp.sum(summed[...].astype(F32), axis=0)
+    _, rows = own_traits.shape
+    half = rows // 2
+    for r in range(RIDGE):
+        for h in range(2):
+            lanes = slice(h * half, (h + 1) * half)
+            at = 8 * r + 4 * h
+            value = own_traits[:, lanes] - pred[at : at + 4]
+            out[r, :, lanes] = value
+            flat[4 * r : 4 * r + 4, lanes] = value
+    out_bf[0] = flat[...].astype(BF16)
+
+
+def residuals(summed, own_traits):
+    share, rows = own_traits.shape
+    vmem = pl.BlockSpec(memory_space=pltpu.VMEM)
+    return pl.pallas_call(
+        residual_kernel,
+        in_specs=[vmem, vmem],
+        out_specs=[vmem, vmem],
+        out_shape=[
+            jax.ShapeDtypeStruct((RIDGE, share, rows), F32),
+            jax.ShapeDtypeStruct((1, RIDGE * share, rows), BF16),
+        ],
+        scratch_shapes=[pltpu.VMEM((RIDGE * share, rows), F32)],
+        compiler_params=pltpu.CompilerParams(vmem_limit_bytes=LIMIT),
+        name="residuals",
+    )(summed, own_traits)
 
 
 def from_sums(sums, dosages, new_dosages, trait_count, count):
@@ -345,19 +400,19 @@
     standard, fresh, between, rhs_shift, slope, square = prepared
 
     core = lax.axis_index("core").astype(jnp.int32).reshape(1)
-    lam = jnp.broadcast_to(jnp.pad(shrink, (0, 3), constant_values=1.0)[:, None], (8, TILE))
-    sent, kept = ridge(
-        core, lam, every, between, rhs_shift, slope[None], square[None], standard, count, depth, padded
+    sent, own = ridge(
+        shrink, core, every, between, rhs_shift, slope[None], square[None], standard, count, depth
     )
 
     arrived = lax.ppermute(sent, "core", [(0, 1), (1, 0)])
-    paired = (kept + arrived.astype(F32)).astype(BF16).reshape(depth, padded, rows)
-    summed = lax.all_to_all(paired, "y", 0, 0, tiled=True)
-    pred = jnp.sum(summed.astype(F32), axis=0)[:used].reshape(RIDGE, share, rows)
-
+    kept = kept_rows(own, standard)
+    paired = (kept.astype(F32) + arrived.astype(F32)).astype(BF16)
+    summed = lax.all_to_all(
+        paired.reshape(depth, paired.shape[0] // depth, rows // 2), "y", 0, 0, tiled=True
+    )
     own_traits = lax.dynamic_slice_in_dim(traits, lax.axis_index(BLK) * share, share, 0)
-    residual = own_traits[None] - pred
-    res_bf = lax.all_gather(residual.astype(BF16).reshape(1, used, rows), BLK, axis=0, tiled=True)
+    residual, res_bf = residuals(summed, own_traits)
+    res_bf = lax.all_gather(res_bf, BLK, axis=0, tiled=True)
     res_bf = res_bf.reshape(blk * used, rows)
     raw_part = dot(res_bf, fresh, ((1,), (0,))).reshape(blk, used, fresh_width)
     res_float = res_bf.astype(F32)
@@ -370,11 +425,11 @@
     ends = jnp.sum(ends, axis=0).reshape(blk // zs, padded, fresh_width)
     sum_sq = ends[:, used, :used]
     scores = ends[:, :used] / jnp.sqrt(count * (sum_sq / count + EPS))[:, :, None]
-    scores = scores.reshape(blk // zs * used, fresh_width)
+    scores = scores.reshape(blk // zs * used, fresh_width).astype(BF16)
     scores = lax.all_to_all(
         jnp.broadcast_to(scores[None], (zs, *scores.shape)), "z", 0, 0, tiled=True
     )
-    scores = scores.reshape(blk, RIDGE, share, fresh_width).transpose(1, 0, 2, 3)
+    scores = scores.astype(F32).reshape(blk, RIDGE, share, fresh_width).transpose(1, 0, 2, 3)
     return residual, scores.reshape(RIDGE, trait_count, fresh_width)
 
 

time: 164 us -> 149 us (0.909)
  blocking collectives: 34.1 us -> 53.1 us
  waiting for transfers between devices: 63.4 us -> 47.4 us
  starting transfers between devices: 34.7 us -> 27.9 us
  other arithmetic: 8.42 us -> 3.91 us
  Pallas kernels: 14.6 us -> 11.8 us
  local copies, waits for them, and re-layouts: 3.61 us -> 1.54 us
    all_to_all x0 -> x2, blocking collectives: none -> 19.2 us  [the longest x1 10.9 us: shards(): lax.all_to_all(jnp.broadcast_to(scores[None], (zs, *scores.shape)), 'z',...]
    all_to_all x3 -> x1, waiting for transfers between devices: 31.2 us -> 14.8 us  [shards(): lax.all_to_all(paired.reshape(depth, paired.shape[0] // depth, rows // 2)...]
    all_to_all x3 -> x1, starting transfers between devices: 14.2 us -> 7.68 us  [shards(): lax.all_to_all(paired.reshape(depth, paired.shape[0] // depth, rows // 2)...]
    pallas_call x1 -> x3, Pallas kernels: 6.54 us -> 4.89 us  [the longest x1 3.42 us: ridge(): pl.pallas_call(functools.partial(ridge_kernel, count, depth), in_specs=[s...]
  transfers between devices with their start and end apart: 6 -> 4, of which waited for: 6 -> 4; matrix products, arithmetic and copies ran while one was open for 4% -> 3% of each run, Pallas kernels for 0% -> 0%
where the time goes in v3:
time: 149 us; the launch traced here: 148 us
  blocking collectives  53.1 us (36%)
  waiting for transfers between devices  47.4 us (32%)
  starting transfers between devices  27.9 us (19%)
  Pallas kernels  11.8 us (8%)
  other arithmetic  3.91 us (3%)
  matrix products  1.83 us (1%)
  local copies, waits for them, and re-layouts  1.54 us (1%)
    all_to_all x1, waiting for transfers between devices, shards(): received = lax.all_to_all(payload, SAMP, 0, 0, tiled=True)  20.1 us
    all_gather x1, blocking collectives, shards(): res_bf = lax.all_gather(res_bf, BLK, axis=0, tiled=True)  18.9 us
    all_to_all x1, blocking collectives, shards(): lax.all_to_all(ends.reshape(zs, blk // zs * padded, fresh_width), 'z', 0,...  15 us
    all_to_all x1, waiting for transfers between devices, shards(): lax.all_to_all(paired.reshape(depth, paired.shape[0] // depth, rows // 2)...  14.8 us
    all_to_all x1, starting transfers between devices, shards(): received = lax.all_to_all(payload, SAMP, 0, 0, tiled=True)  13.2 us
    all_to_all x1, waiting for transfers between devices, shards(): every = lax.all_to_all(own_rows, SAMP, 0, 0, tiled=True)  11.4 us
    all_to_all x1, blocking collectives, shards(): lax.all_to_all(jnp.broadcast_to(scores[None], (zs, *scores.shape)), 'z',...  10.9 us
    all_to_all x1, blocking collectives, shards(): lax.all_to_all(jnp.broadcast_to(ends[None], (xs, *ends.shape)), 'x', 0, 0...  8.26 us
  transfers between devices with their start and end apart: 4, of which 4 were waited for; matrix products, arithmetic and copies ran while one was open for 3% of the time, Pallas kernels for 0%

profile of v3, /device:TPU:8, one launch (start us, length us, event | category | flops | bytes accessed | tf_op | source)
XLA Modules:
  0.0 148.4 jit_solution(3779408152462607386)
XLA Ops:
  0.6 6.0 %products.1 = bf16[32,8,1280]{2,1,0:T(8,128)(2,1)} custom-call(s32[1536,512]{1,0:T(8,128)} %dosages.1, s32[1536,128]{1,0:T(8,128)} %new_dosages.1, f32[64,1536]{1,0:T(8,128)} %traits.1), custom_call_target="tpu_custom_call" | custom-call | tf_op jit(solution)/shard_map/products/pallas_call | solution.py:134
  6.7 13.2 %all-to-all-start = ((bf16[32,8,1280]{2,1,0:T(8,128)(2,1)}), bf16[32,8,1280]{2,1,0:T(8,128)(2,1)S(1)}, u32[]{:S(2)}, u32[]{:S(2)}) async-start(bf16[32,8,1280]{2,1,0:T(8,128)(2,1)} %products.1), calls=%async_computation | async-start | bytes 1310720 | tf_op jit(solution)/shard_map/all_to_all | solution.py:396
  19.8 20.1 %all-to-all-done.received = bf16[32,8,1280]{2,1,0:T(8,128)(2,1)S(1)} async-done(((bf16[32,8,1280]{2,1,0:T(8,128)(2,1)}), bf16[32,8,1280]{2,1,0:T(8,128)(2,1)S(1)}, u32[]{:S(2)}, u32[]{:S(2)}) %all-to-all-start) | async-done | bytes 655392 | tf_op jit(solution)/shard_map/all_to_all | solution.py:396
  40.0 0.9 owner.1
  40.9 0.1 reduce_sum.36
  41.0 5.2 %all-to-all-start.1 = ((bf16[32,8,896]{2,1,0:T(8,128)(2,1)}), bf16[32,8,896]{2,1,0:T(8,128)(2,1)S(1)}, u32[]{:S(2)}, u32[]{:S(2)}) async-start(bf16[32,8,896]{2,1,0:T(8,128)(2,1)} %get-tuple-element.8), calls=%async_computation.1 | async-start | bytes 917504 | tf_op jit(solution)/shard_map/all_to_all | solution.py:398
  46.2 0.3 fusion.rhs_shift
  46.6 1.0 convolution_multiply_fusion.between
  47.6 0.0 copy-start
  47.6 2.3 %multiply_convert_fusion.standard = bf16[1536,512]{1,0:T(8,128)(2,1)S(1)} fusion(s32[1536,512]{1,0:T(8,128)} %dosages.1, f32[512]{0:T(512)S(1)} %get-tuple-element.15, f32[512]{0:T(512)S(1)} %get-tuple-element.18), kind=kLoop, calls=%fused_computation | loop fusion | flops 3145728 | bytes 4722688 | tf_op jit(solution)/shard_map/convert_element_type | solution.py:186
  50.0 11.4 %all-to-all-done.1.every = bf16[32,8,896]{2,1,0:T(8,128)(2,1)S(1)} async-done(((bf16[32,8,896]{2,1,0:T(8,128)(2,1)}), bf16[32,8,896]{2,1,0:T(8,128)(2,1)S(1)}, u32[]{:S(2)}, u32[]{:S(2)}) %all-to-all-start.1) | async-done | bytes 458784 | tf_op jit(solution)/shard_map/all_to_all | solution.py:398
  61.3 0.0 copy-done
  61.3 3.4 %ridge.1 = (bf16[320,768]{1,0:T(8,128)(2,1)S(1)}, bf16[320,512]{1,0:T(8,128)(2,1)S(1)}) custom-call(f32[5]{0:T(128)S(1)} %copy-done, s32[1]{0:T(128)} %bitcast.core, bf16[32,8,896]{2,1,0:T(8,128)(2,1)S(1)} %all-to-all-done.1.every, f32[512,512]{1,0:T(8,128)S(1)} %convolution_multiply_fusion.between, f32[64,512]{1,0:T(8,128)S(1)} %fusion.rhs_shift, ...), custom_call_target="tpu_custom_call" | custom-call | tf_op jit(solution)/shard_map/ridge/pallas_call | solution.py:295
  64.8 1.9 %collective-permute-start = (bf16[320,768]{1,0:T(8,128)(2,1)S(1)}, bf16[320,768]{1,0:T(8,128)(2,1)S(1)}, u32[]{:S(2)}, u32[]{:S(2)}) collective-permute-start(bf16[320,768]{1,0:T(8,128)(2,1)S(1)} %get-tuple-element.11), channel_id=1, source_target_pairs={{0,1},{1,0},{2,3},{3,2},{4,5},{5,4},{6,7},{7,6},{8,9},{9,8},{10,11... | collective-permute-start | bytes 1474568 | tf_op jit(solution)/shard_map/ppermute | solution.py:407
  66.7 0.7 kept.1
  67.4 1.1 collective-permute-done
  68.5 0.9 add_convert_fusion
  69.4 0.0 copy-start.1
  69.4 7.7 %all-to-all-start.2 = ((bf16[8,40,768]{2,1,0:T(8,128)(2,1)}), bf16[8,40,768]{2,1,0:T(8,128)(2,1)S(1)}, u32[]{:S(2)}, u32[]{:S(2)}) async-start(bf16[8,40,768]{2,1,0:T(8,128)(2,1)} %bitcast.7), calls=%async_computation.2 | async-start | bytes 983040 | tf_op jit(solution)/shard_map/all_to_all | solution.py:410
  77.1 0.8 constant_dynamic-slice_fusion.own_traits
  77.9 14.8 %all-to-all-done.2.summed = bf16[8,40,768]{2,1,0:T(8,128)(2,1)S(1)} async-done(((bf16[8,40,768]{2,1,0:T(8,128)(2,1)}), bf16[8,40,768]{2,1,0:T(8,128)(2,1)S(1)}, u32[]{:S(2)}, u32[]{:S(2)}) %all-to-all-start.2) | async-done | bytes 491552 | tf_op jit(solution)/shard_map/all_to_all | solution.py:410
  92.7 0.8 residuals.1
  93.5 18.9 %all_gather.3 = bf16[16,20,1536]{2,1,0:T(8,128)(2,1)S(1)} all-gather(bf16[1,20,1536]{2,1,0:T(8,128)(2,1)S(1)} %get-tuple-element.13), channel_id=1, replica_groups=mesh['x'=4,'z'=8,'y'=8,'core'=2] {'y','core'}, dimensions={0}, use_global_device_ids=true | all-gather | bytes 1044480 | tf_op jit(solution)/shard_map/all_gather | solution.py:415
  112.4 0.3 multiply_reduce_fusion
  112.8 0.0 copy-done.1
  112.8 0.5 fusion.2
  113.3 15.0 %all_to_all.30 = f32[8,48,128]{2,1,0:T(8,128)S(1)} all-to-all(f32[8,48,128]{2,1,0:T(8,128)S(1)} %bitcast.87), channel_id=1, replica_groups=mesh['x'=4,'z'=8,'y'=8,'core'=2] {'z'}, dimensions={0} | all-to-all | bytes 393216 | tf_op jit(solution)/shard_map/all_to_all | solution.py:422
  128.3 8.3 %all_to_all.31 = f32[4,48,128]{2,1,0:T(8,128)S(1)} all-to-all(f32[4,48,128]{2,1,0:T(8,128)S(1)} %broadcast_in_dim.4), channel_id=1, replica_groups=mesh['x'=4,'z'=8,'y'=8,'core'=2] {'x'}, dimensions={0} | all-to-all | bytes 196608 | tf_op jit(solution)/shard_map/all_to_all | solution.py:424
  136.6 0.1 fusion.10
  136.7 10.9 %all_to_all.32 = bf16[8,40,128]{2,1,0:T(8,128)(2,1)S(1)} all-to-all(bf16[8,40,128]{2,1,0:T(8,128)(2,1)S(1)} %broadcast_in_dim.5), channel_id=1, replica_groups=mesh['x'=4,'z'=8,'y'=8,'core'=2] {'z'}, dimensions={0} | all-to-all | bytes 163840 | tf_op jit(solution)/shard_map/all_to_all | solution.py:429
  147.7 0.7 copy.9
  (16 shorter events, 0.2 us)
Async XLA Ops:
  6.7 33.3 %all-to-all-start = ((bf16[32,8,1280]{2,1,0:T(8,128)(2,1)}), bf16[32,8,1280]{2,1,0:T(8,128)(2,1)S(1)}, u32[]{:S(2)}, u32[]{:S(2)}) async-start(bf16[32,8,1280]{2,1,0:T(8,128)(2,1)} %products.1), calls=%async_computation | async-start | bytes 1310720 | tf_op jit(solution)/shard_map/all_to_all | solution.py:396
  41.0 20.3 %all-to-all-start.1 = ((bf16[32,8,896]{2,1,0:T(8,128)(2,1)}), bf16[32,8,896]{2,1,0:T(8,128)(2,1)S(1)}, u32[]{:S(2)}, u32[]{:S(2)}) async-start(bf16[32,8,896]{2,1,0:T(8,128)(2,1)} %get-tuple-element.8), calls=%async_computation.1 | async-start | bytes 917504 | tf_op jit(solution)/shard_map/all_to_all | solution.py:398
  47.6 13.7 %copy-start = (f32[5]{0:T(128)S(1)}, f32[5]{0:T(128)}, u32[]{:S(2)}) copy-start(f32[5]{0:T(128)} %lam.1) | copy-start | bytes 64
  64.8 3.8 %collective-permute-start = (bf16[320,768]{1,0:T(8,128)(2,1)S(1)}, bf16[320,768]{1,0:T(8,128)(2,1)S(1)}, u32[]{:S(2)}, u32[]{:S(2)}) collective-permute-start(bf16[320,768]{1,0:T(8,128)(2,1)S(1)} %get-tuple-element.11), channel_id=1, source_target_pairs={{0,1},{1,0},{2,3},{3,2},{4,5},{5,4},{6,7},{7,6},{8,9},{9,8},{10,11... | collective-permute-start | bytes 1474568 | tf_op jit(solution)/shard_map/ppermute | solution.py:407
  69.4 43.4 %copy-start.1 = (s32[1536,128]{1,0:T(8,128)S(1)}, s32[1536,128]{1,0:T(8,128)}, u32[]{:S(2)}) copy-start(s32[1536,128]{1,0:T(8,128)} %new_dosages.1) | copy-start | bytes 2359300
  69.4 23.3 %all-to-all-start.2 = ((bf16[8,40,768]{2,1,0:T(8,128)(2,1)}), bf16[8,40,768]{2,1,0:T(8,128)(2,1)S(1)}, u32[]{:S(2)}, u32[]{:S(2)}) async-start(bf16[8,40,768]{2,1,0:T(8,128)(2,1)} %bitcast.7), calls=%async_computation.2 | async-start | bytes 983040 | tf_op jit(solution)/shard_map/all_to_all | solution.py:410

commit v4 on v3

--- a/solution.py
+++ b/solution.py
@@ -86,10 +86,21 @@
 
     @pl.when(step == pl.num_programs(0) - 1)
     def _():
-        local = sums[:8]
-        shift = 1.0 / (8.0 * rows)
-        gram[...] = gram[...] - dot(local, local, over_rows, EXACT) * shift
-        cross[...] = cross[...] - dot(trait_sums[...], local, over_rows, EXACT) * shift
+        shift = 1.0 / rows
+        local, line = sums[:8], lax.broadcasted_iota(jnp.int32, (8, width), 0)
+        high = rounded_in_kernel(local)
+        left = jnp.where(line < 4, jnp.where((line & 1) == 0, high, local - high), 0.0).astype(BF16)
+        right = jnp.where(line < 2, high, local - high).astype(BF16)
+        gram[:half, :] = gram[:half, :] - dot(left[:, :half], right, over_rows) * shift
+        gram[half:, half:] = gram[half:, half:] - dot(left[:, half:], right[:, half:], over_rows) * shift
+        top = rounded_in_kernel(trait_sums[...])
+        middle = rounded_in_kernel(trait_sums[...] - top)
+        bottom = trait_sums[...] - top - middle
+        spot = lax.broadcasted_iota(jnp.int32, top.shape, 0)
+        left = jnp.where((spot == 0) | (spot == 3), top, jnp.where((spot == 1) | (spot == 4), middle, bottom))
+        left = jnp.where(spot < 6, left, 0.0).astype(BF16)
+        right = jnp.where(line < 3, high, local - high).astype(BF16)
+        cross[...] = cross[...] - dot(left, right, over_rows) * shift
         gram_places, cross_places = places(width, trait_count, samp)
         for row, column, owner, place in gram_tiles(width, samp):
             out[owner, :, place * TILE : (place + 1) * TILE] = gram[
@@ -249,13 +260,21 @@
     matrix = jnp.where(same, 0.0, matrix)
     rhs = cross[...] * (1.0 / count) * scale + rhs_shift[...]
 
+    parts, sizes = split(matrix), split(jnp.abs(matrix))
+
+    def product(values, high, low):
+        count = values.shape[0]
+        top, bottom = split(values)
+        out = dot(jnp.concatenate([top, bottom], axis=0), high, ((1,), (0,)))
+        return out[:count] + out[count:] + dot(top, low, ((1,), (0,)))
+
     def apply_gram(values):
-        return dot(values * scale, matrix, ((1,), (0,)), EXACT) * scale + diagonal * values
+        return product(values * scale, *parts) * scale + diagonal * values
 
     once = apply_gram(rhs)
     twice = apply_gram(once)
     eight = jnp.broadcast_to(scale, (8, width))
-    column_sums = dot(eight, jnp.abs(matrix), ((1,), (0,)), EXACT)[0:1] * scale + diagonal
+    column_sums = product(eight, *sizes)[0:1] * scale + diagonal
     bound = jnp.max(column_sums, axis=1, keepdims=True)
     powers = [(v, swapped_tiles(v)) for v in (rhs, once, twice)]
     for r in range(RIDGE):

time: 149 us -> 147 us (0.987)
  Pallas kernels: 11.8 us -> 9.93 us
where the time goes in v4:
time: 147 us
  blocking collectives  53.1 us (36%)
  waiting for transfers between devices  47.4 us (32%)
  starting transfers between devices  27.9 us (19%)
  Pallas kernels  9.93 us (7%)
  other arithmetic  3.91 us (3%)
  matrix products  1.82 us (1%)
  local copies, waits for them, and re-layouts  1.54 us (1%)
    all_to_all x1, waiting for transfers between devices, shards(): received = lax.all_to_all(payload, SAMP, 0, 0, tiled=True)  20.1 us
    all_gather x1, blocking collectives, shards(): res_bf = lax.all_gather(res_bf, BLK, axis=0, tiled=True)  18.9 us
    all_to_all x1, blocking collectives, shards(): lax.all_to_all(ends.reshape(zs, blk // zs * padded, fresh_width), 'z', 0,...  15 us
    all_to_all x1, waiting for transfers between devices, shards(): lax.all_to_all(paired.reshape(depth, paired.shape[0] // depth, rows // 2)...  14.8 us
    all_to_all x1, starting transfers between devices, shards(): received = lax.all_to_all(payload, SAMP, 0, 0, tiled=True)  13.2 us
    all_to_all x1, waiting for transfers between devices, shards(): every = lax.all_to_all(own_rows, SAMP, 0, 0, tiled=True)  11.4 us
    all_to_all x1, blocking collectives, shards(): lax.all_to_all(jnp.broadcast_to(scores[None], (zs, *scores.shape)), 'z',...  10.9 us
    all_to_all x1, blocking collectives, shards(): lax.all_to_all(jnp.broadcast_to(ends[None], (xs, *ends.shape)), 'x', 0, 0...  8.26 us
  transfers between devices with their start and end apart: 4, of which 4 were waited for; matrix products, arithmetic and copies ran while one was open for 3% of the time, Pallas kernels for 0%

profile of v4, /device:TPU:8, one launch (start us, length us, event | category | flops | bytes accessed | tf_op | source)
XLA Modules:
  0.0 146.5 jit_solution(10271381009896761517)
XLA Ops:
  0.6 5.2 %products.1 = bf16[32,8,1280]{2,1,0:T(8,128)(2,1)} custom-call(s32[1536,512]{1,0:T(8,128)} %dosages.1, s32[1536,128]{1,0:T(8,128)} %new_dosages.1, f32[64,1536]{1,0:T(8,128)} %traits.1), custom_call_target="tpu_custom_call" | custom-call | tf_op jit(solution)/shard_map/products/pallas_call | solution.py:145
  5.8 13.2 %all-to-all-start = ((bf16[32,8,1280]{2,1,0:T(8,128)(2,1)}), bf16[32,8,1280]{2,1,0:T(8,128)(2,1)S(1)}, u32[]{:S(2)}, u32[]{:S(2)}) async-start(bf16[32,8,1280]{2,1,0:T(8,128)(2,1)} %products.1), calls=%async_computation | async-start | bytes 1310720 | tf_op jit(solution)/shard_map/all_to_all | solution.py:415
  19.0 20.1 %all-to-all-done.received = bf16[32,8,1280]{2,1,0:T(8,128)(2,1)S(1)} async-done(((bf16[32,8,1280]{2,1,0:T(8,128)(2,1)}), bf16[32,8,1280]{2,1,0:T(8,128)(2,1)S(1)}, u32[]{:S(2)}, u32[]{:S(2)}) %all-to-all-start) | async-done | bytes 655392 | tf_op jit(solution)/shard_map/all_to_all | solution.py:415
  39.1 0.9 owner.1
  40.0 0.1 reduce_sum.36
  40.2 5.2 %all-to-all-start.1 = ((bf16[32,8,896]{2,1,0:T(8,128)(2,1)}), bf16[32,8,896]{2,1,0:T(8,128)(2,1)S(1)}, u32[]{:S(2)}, u32[]{:S(2)}) async-start(bf16[32,8,896]{2,1,0:T(8,128)(2,1)} %get-tuple-element.8), calls=%async_computation.1 | async-start | bytes 917504 | tf_op jit(solution)/shard_map/all_to_all | solution.py:417
  45.3 0.3 fusion.rhs_shift
  45.7 1.0 convolution_multiply_fusion.between
  46.7 0.0 copy-start
  46.7 2.3 %multiply_convert_fusion.standard = bf16[1536,512]{1,0:T(8,128)(2,1)S(1)} fusion(s32[1536,512]{1,0:T(8,128)} %dosages.1, f32[512]{0:T(512)S(1)} %get-tuple-element.15, f32[512]{0:T(512)S(1)} %get-tuple-element.18), kind=kLoop, calls=%fused_computation | loop fusion | flops 3145728 | bytes 4722688 | tf_op jit(solution)/shard_map/convert_element_type | solution.py:197
  49.1 11.4 %all-to-all-done.1.every = bf16[32,8,896]{2,1,0:T(8,128)(2,1)S(1)} async-done(((bf16[32,8,896]{2,1,0:T(8,128)(2,1)}), bf16[32,8,896]{2,1,0:T(8,128)(2,1)S(1)}, u32[]{:S(2)}, u32[]{:S(2)}) %all-to-all-start.1) | async-done | bytes 458784 | tf_op jit(solution)/shard_map/all_to_all | solution.py:417
  60.5 0.0 copy-done
  60.5 2.4 %ridge.1 = (bf16[320,768]{1,0:T(8,128)(2,1)S(1)}, bf16[320,512]{1,0:T(8,128)(2,1)S(1)}) custom-call(f32[5]{0:T(128)S(1)} %copy-done, s32[1]{0:T(128)} %bitcast.core, bf16[32,8,896]{2,1,0:T(8,128)(2,1)S(1)} %all-to-all-done.1.every, f32[512,512]{1,0:T(8,128)S(1)} %convolution_multiply_fusion.between, f32[64,512]{1,0:T(8,128)S(1)} %fusion.rhs_shift, ...), custom_call_target="tpu_custom_call" | custom-call | tf_op jit(solution)/shard_map/ridge/pallas_call | solution.py:314
  62.9 1.9 %collective-permute-start = (bf16[320,768]{1,0:T(8,128)(2,1)S(1)}, bf16[320,768]{1,0:T(8,128)(2,1)S(1)}, u32[]{:S(2)}, u32[]{:S(2)}) collective-permute-start(bf16[320,768]{1,0:T(8,128)(2,1)S(1)} %get-tuple-element.11), channel_id=1, source_target_pairs={{0,1},{1,0},{2,3},{3,2},{4,5},{5,4},{6,7},{7,6},{8,9},{9,8},{10,11... | collective-permute-start | bytes 1474568 | tf_op jit(solution)/shard_map/ppermute | solution.py:426
  64.8 0.7 kept.1
  65.5 1.1 collective-permute-done
  66.6 0.9 add_convert_fusion
  67.5 0.0 copy-start.1
  67.5 7.7 %all-to-all-start.2 = ((bf16[8,40,768]{2,1,0:T(8,128)(2,1)}), bf16[8,40,768]{2,1,0:T(8,128)(2,1)S(1)}, u32[]{:S(2)}, u32[]{:S(2)}) async-start(bf16[8,40,768]{2,1,0:T(8,128)(2,1)} %bitcast.7), calls=%async_computation.2 | async-start | bytes 983040 | tf_op jit(solution)/shard_map/all_to_all | solution.py:429
  75.2 0.8 constant_dynamic-slice_fusion.own_traits
  76.0 14.8 %all-to-all-done.2.summed = bf16[8,40,768]{2,1,0:T(8,128)(2,1)S(1)} async-done(((bf16[8,40,768]{2,1,0:T(8,128)(2,1)}), bf16[8,40,768]{2,1,0:T(8,128)(2,1)S(1)}, u32[]{:S(2)}, u32[]{:S(2)}) %all-to-all-start.2) | async-done | bytes 491552 | tf_op jit(solution)/shard_map/all_to_all | solution.py:429
  90.8 0.8 residuals.1
  91.6 18.9 %all_gather.3 = bf16[16,20,1536]{2,1,0:T(8,128)(2,1)S(1)} all-gather(bf16[1,20,1536]{2,1,0:T(8,128)(2,1)S(1)} %get-tuple-element.13), channel_id=1, replica_groups=mesh['x'=4,'z'=8,'y'=8,'core'=2] {'y','core'}, dimensions={0}, use_global_device_ids=true | all-gather | bytes 1044480 | tf_op jit(solution)/shard_map/all_gather | solution.py:434
  110.6 0.3 multiply_reduce_fusion
  110.9 0.0 copy-done.1
  110.9 0.5 fusion.2
  111.4 15.0 %all_to_all.30 = f32[8,48,128]{2,1,0:T(8,128)S(1)} all-to-all(f32[8,48,128]{2,1,0:T(8,128)S(1)} %bitcast.87), channel_id=1, replica_groups=mesh['x'=4,'z'=8,'y'=8,'core'=2] {'z'}, dimensions={0} | all-to-all | bytes 393216 | tf_op jit(solution)/shard_map/all_to_all | solution.py:441
  126.4 8.3 %all_to_all.31 = f32[4,48,128]{2,1,0:T(8,128)S(1)} all-to-all(f32[4,48,128]{2,1,0:T(8,128)S(1)} %broadcast_in_dim.4), channel_id=1, replica_groups=mesh['x'=4,'z'=8,'y'=8,'core'=2] {'x'}, dimensions={0} | all-to-all | bytes 196608 | tf_op jit(solution)/shard_map/all_to_all | solution.py:443
  134.7 0.1 fusion.10
  134.9 10.9 %all_to_all.32 = bf16[8,40,128]{2,1,0:T(8,128)(2,1)S(1)} all-to-all(bf16[8,40,128]{2,1,0:T(8,128)(2,1)S(1)} %broadcast_in_dim.5), channel_id=1, replica_groups=mesh['x'=4,'z'=8,'y'=8,'core'=2] {'z'}, dimensions={0} | all-to-all | bytes 163840 | tf_op jit(solution)/shard_map/all_to_all | solution.py:448
  145.8 0.7 copy.9
  (16 shorter events, 0.2 us)
Async XLA Ops:
  5.8 33.3 %all-to-all-start = ((bf16[32,8,1280]{2,1,0:T(8,128)(2,1)}), bf16[32,8,1280]{2,1,0:T(8,128)(2,1)S(1)}, u32[]{:S(2)}, u32[]{:S(2)}) async-start(bf16[32,8,1280]{2,1,0:T(8,128)(2,1)} %products.1), calls=%async_computation | async-start | bytes 1310720 | tf_op jit(solution)/shard_map/all_to_all | solution.py:415
  40.2 20.3 %all-to-all-start.1 = ((bf16[32,8,896]{2,1,0:T(8,128)(2,1)}), bf16[32,8,896]{2,1,0:T(8,128)(2,1)S(1)}, u32[]{:S(2)}, u32[]{:S(2)}) async-start(bf16[32,8,896]{2,1,0:T(8,128)(2,1)} %get-tuple-element.8), calls=%async_computation.1 | async-start | bytes 917504 | tf_op jit(solution)/shard_map/all_to_all | solution.py:417
  46.7 13.7 %copy-start = (f32[5]{0:T(128)S(1)}, f32[5]{0:T(128)}, u32[]{:S(2)}) copy-start(f32[5]{0:T(128)} %lam.1) | copy-start | bytes 64
  62.9 3.8 %collective-permute-start = (bf16[320,768]{1,0:T(8,128)(2,1)S(1)}, bf16[320,768]{1,0:T(8,128)(2,1)S(1)}, u32[]{:S(2)}, u32[]{:S(2)}) collective-permute-start(bf16[320,768]{1,0:T(8,128)(2,1)S(1)} %get-tuple-element.11), channel_id=1, source_target_pairs={{0,1},{1,0},{2,3},{3,2},{4,5},{5,4},{6,7},{7,6},{8,9},{9,8},{10,11... | collective-permute-start | bytes 1474568 | tf_op jit(solution)/shard_map/ppermute | solution.py:426
  67.5 43.4 %copy-start.1 = (s32[1536,128]{1,0:T(8,128)S(1)}, s32[1536,128]{1,0:T(8,128)}, u32[]{:S(2)}) copy-start(s32[1536,128]{1,0:T(8,128)} %new_dosages.1) | copy-start | bytes 2359300
  67.5 23.3 %all-to-all-start.2 = ((bf16[8,40,768]{2,1,0:T(8,128)(2,1)}), bf16[8,40,768]{2,1,0:T(8,128)(2,1)S(1)}, u32[]{:S(2)}, u32[]{:S(2)}) async-start(bf16[8,40,768]{2,1,0:T(8,128)(2,1)} %bitcast.7), calls=%async_computation.2 | async-start | bytes 983040 | tf_op jit(solution)/shard_map/all_to_all | solution.py:429
